TPU v7x, 512 devices: a whole 4x4x16 slice. The times are simulated.
512 devices in a mesh: gx: 16 (over z), gy: 8 (over y, core), gz: 4 (over x).
Axes of the slice: x: 4, y: 4, z: 16, core: 2. Of those that a mesh axis runs over, the one named last changes fastest.
Arguments:
- right_side: float32 [256, 128, 512], P('gx', 'gy', 'gz'), may hold values from -6 to 6
- conductivity: float32 [256, 128, 512], P('gx', 'gy', 'gz'), may hold values from 0.3 to 3
Outputs:
- solution_field: float32 [256, 128, 512], P('gx', 'gy', 'gz')
All inputs are finite; a program needn't handle non-finite values.
Results may differ from a plain program's by a relative error of at most 0.0001.
Values sent between devices are 32-bit elements; how exact they have to be, the bound alone decides.
No kernel may reach another device: no remote copies, remote signals or barrier semaphores. Data moves between devices by JAX's collectives and lax.ppermute only.
A program may use at most 64 MiB of HBM per device.

v0:
```python
import jax
import jax.numpy as jnp
from jax import lax
from jax.experimental import pallas as pl
from jax.experimental.pallas import tpu as pltpu
from jax.sharding import PartitionSpec as P

F_HALO = 12
B_HALO = 13
BLOCK = 16
F_PLANES = BLOCK + 2 * F_HALO
B_PLANES = BLOCK + 2 * B_HALO
PLANES = F_PLANES + B_PLANES
GROUPS = -(-PLANES // 8)
F_GROUPS = F_PLANES // 8
ROWS = 48
COARSE_SWEEPS = 8
F32 = jnp.float32


def iota(shape, dim):
    return lax.broadcasted_iota(jnp.int32, shape, dim)


def split_matmul(value, selector):
    high = value.astype(jnp.bfloat16)
    low = (value - high.astype(F32)).astype(jnp.bfloat16)
    return jnp.dot(high, selector, preferred_element_type=F32) + jnp.dot(
        low, selector, preferred_element_type=F32
    )


def selector_of(condition):
    return jnp.where(condition, 1.0, 0.0).astype(jnp.bfloat16)


def pair_selector(source_lanes, first, out_lanes, offset, count):
    source = iota((source_lanes, out_lanes), 0) - first
    target = iota((source_lanes, out_lanes), 1) - offset
    return selector_of(
        (source >= 0) & (source < 2 * count) & ((source >> 1) == target)
    )


def spread_selector(first, offset, count):
    source = iota((128, 128), 0) - first
    target = iota((128, 128), 1) - offset
    return selector_of((source >= 0) & (source < count) & ((target >> 1) == source))


class Level:
    names = ("b", "g", "fx", "fy", "fz", "d", "ir", "ik", "r", "k")

    def __init__(self, refs, columns, walled):
        self.walled = walled
        self.columns = columns
        for index, name in enumerate(self.names):
            setattr(self, name, refs[index * columns : (index + 1) * columns])
        self.lane = iota((8, 128), 1)
        self.parity = (iota((8, 128), 0) + self.lane) & 1

    @staticmethod
    def scratch(columns, planes, rows):
        return [(planes, rows + 16, 128)] * (len(Level.names) * columns)

    def at(self, refs, plane, row):
        return [ref[plane, row : row + 8] for ref in refs]

    def put(self, refs, plane, row, values):
        for ref, value in zip(refs, values):
            ref[plane, row : row + 8] = value

    def turn(self, values, step):
        rolled = [pltpu.roll(value, 127 if step > 0 else 1, 1) for value in values]
        if self.columns == 1:
            return rolled
        edge = self.lane == (127 if step > 0 else 0)
        first, second = rolled
        return [jnp.where(edge, second, first), jnp.where(edge, first, second)]

    def clear(self, planes, rows, ends):
        zero = jnp.zeros((8, 128), F32)
        for refs in (self.b, self.fy, self.r, self.k):
            for ref in refs:

                @pl.loop(0, planes)
                def _(plane):
                    ref[plane, 0:8] = zero
                    ref[plane, rows + 8 : rows + 16] = zero

        for refs in (self.r, self.k):
            for ref in refs:
                for plane in ends:
                    ref[plane] = jnp.zeros((rows + 16, 128), F32)

    def before(self, plane, rows):
        for row in range(8, rows + 8, 8):
            near = zip(self.at(self.b, plane, row), self.at(self.b, plane + 1, row))
            self.put(self.fx, plane, row, [own + other for own, other in near])

    def setup(self, plane, rows, red):
        for row in range(8, rows + 8, 8):
            b = self.at(self.b, plane, row)
            x_low, x_high = self.at(self.b, plane - 1, row), self.at(self.b, plane + 1, row)
            y_low, y_high = self.at(self.b, plane, row - 1), self.at(self.b, plane, row + 1)
            z_low, z_high = self.turn(b, -1), self.turn(b, 1)
            g = self.at(self.g, plane, row)
            for column in range(self.columns):
                own, z_before, z_after = b[column], z_low[column], z_high[column]
                face = own + z_after
                if self.walled:
                    z_before = jnp.where(self.lane > 0, z_before, 0.0)
                    z_after = jnp.where(self.lane < 127, z_after, 0.0)
                    face = jnp.where(self.lane < 127, face, 0.0)
                total = (6.0 * own + (x_low[column] + x_high[column])) + (
                    (y_low[column] + y_high[column]) + (z_before + z_after)
                )
                inside = own > 0.0
                inverse = 1.0 / jnp.where(inside, total, 1.0)
                first = self.parity == red
                reds = jnp.where(inside & first, inverse, 0.0)
                here = (plane, slice(row, row + 8))
                self.fx[column][here] = own + x_high[column]
                self.fy[column][here] = own + y_high[column]
                self.fz[column][here] = face
                self.d[column][here] = total
                self.ir[column][here] = reds
                self.ik[column][here] = jnp.where(inside & ~first, inverse, 0.0)
                self.r[column][here] = g[column] * reds
                self.k[column][here] = jnp.zeros((8, 128), F32)

    def total(self, source, plane, row):
        v = self.at(source, plane, row)
        face_z = self.at(self.fz, plane, row)
        z_high = self.turn(v, 1)
        z_low = self.turn([face * value for face, value in zip(face_z, v)], -1)
        out = []
        for column in range(self.columns):
            ref, fx, fy = source[column], self.fx[column], self.fy[column]
            here = slice(row, row + 8)
            along_x = (
                fx[plane, here] * ref[plane + 1, here]
                + fx[plane - 1, here] * ref[plane - 1, here]
            )
            low, high = slice(row - 1, row + 7), slice(row + 1, row + 9)
            along_y = fy[plane, here] * ref[plane, high] + fy[plane, low] * ref[plane, low]
            along_z = face_z[column] * z_high[column] + z_low[column]
            out.append((self.g[column][plane, here] + along_x) + (along_y + along_z))
        return out

    def relax(self, step, plane, rows):
        source, inverse, target = (
            (self.r, self.ik, self.k),
            (self.k, self.ir, self.r),
            (self.r, self.ik, self.k),
        )[step]
        results = []
        for row in rows:
            values = self.total(source, plane, row)
            scale = self.at(inverse, plane, row)
            values = [value * factor for value, factor in zip(values, scale)]
            if step == 2:
                values = [a + b for a, b in zip(values, self.at(self.r, plane, row))]
            results.append(values)
        for row, values in zip(rows, results):
            self.put(target, plane, row, values)

    def rest(self, plane, row):
        values = self.total(self.k, plane, row)
        out = []
        for column, value in enumerate(values):
            here = (plane, slice(row, row + 8))
            value = value - self.d[column][here] * self.k[column][here]
            out.append(jnp.where(self.b[column][here] > 0.0, value, 0.0))
        return out


def halves(ref, rows):
    return ref[pl.ds(0, rows, stride=2), :] + ref[pl.ds(1, rows, stride=2), :]


def pack_kernel(f_ref, b_ref, low_ref, high_ref, main_ref, left_ref, right_ref):
    lane = iota((BLOCK, 128), 1)

    def source(index):
        if index < F_HALO:
            return low_ref[index]
        if index < F_HALO + BLOCK:
            return f_ref[index - F_HALO]
        if index < F_PLANES:
            return high_ref[index - F_HALO - BLOCK]
        index -= F_PLANES
        if index < B_HALO:
            return low_ref[F_HALO + index]
        if index < B_HALO + BLOCK:
            return b_ref[index - B_HALO]
        return high_ref[F_HALO + index - B_HALO - BLOCK]

    for group in range(GROUPS):
        left = jnp.zeros((BLOCK, 128), F32)
        right = jnp.zeros((BLOCK, 128), F32)
        for slot in range(8):
            index = group * 8 + slot
            if index >= PLANES:
                break
            plane = source(index)
            main_ref[index] = plane
            turned = pltpu.roll(plane, 16 * slot, 1) if slot else plane
            left = jnp.where((lane >> 4) == slot, turned, left)
            right = jnp.where((lane >> 4) == ((slot - 1) & 7), turned, right)
        left_ref[group] = left
        right_ref[group] = right


def fine_kernel(low_ref, own_ref, high_ref, u0_ref, u1_ref, coarse_ref, *scratch):
    count = len(Level.names)
    fine = Level(scratch[: 2 * count], 2, False)
    middle = Level(scratch[2 * count : 3 * count], 1, False)
    rest_main, rest_side, sum_main, sum_side, collect = scratch[3 * count :]

    lane = iota((BLOCK, 128), 1)
    even = ((lane >> 4) & 1) == 0
    edges = (lane < 16) | (lane >= 112)

    def place(target, first, group, slots, scale):
        for part, source in enumerate((low_ref, own_ref, high_ref)):
            after, before = source[PLANES + group], source[PLANES + GROUPS + group]
            merged = (jnp.where(even, after, before), jnp.where(even, before, after))
            rows = slice(8 + BLOCK * part, 8 + BLOCK * part + BLOCK)
            for slot in slots:
                side = merged[slot & 1]
                if slot:
                    side = pltpu.roll(side, 128 - 16 * slot, 1)
                side = jnp.where(edges, side, 0.0)
                plane = source[group * 8 + slot]
                if scale != 1.0:
                    side, plane = side * scale, plane * scale
                target[0][first + slot, rows] = plane
                target[1][first + slot, rows] = side

    @pl.loop(0, F_GROUPS)
    def _(group):
        place(fine.g, group * 8 + 1, group, range(8), 2.0)

    @pl.loop(F_GROUPS, GROUPS - 1)
    def _(group):
        place(fine.b, group * 8 - F_PLANES, group, range(8), 1.0)

    group = GROUPS - 1
    place(fine.b, group * 8 - F_PLANES, group, range(PLANES - 8 * group), 1.0)

    fine.clear(B_PLANES, ROWS, (0, B_PLANES - 1))
    fine.before(0, ROWS)

    @pl.loop(1, B_PLANES - 1, step=2)
    def _(plane):
        fine.setup(plane, ROWS, 0)
        fine.setup(plane + 1, ROWS, 1)

    every = range(8, ROWS + 8, 8)
    inner = range(16, ROWS, 8)
    for step in range(3):
        beside = 2 - step
        near = B_HALO - beside

        @pl.loop(near, near + BLOCK + 2 * beside, step=2)
        def _(plane):
            fine.relax(step, plane, every)
            fine.relax(step, plane + 1, every)

        @pl.loop(near - 9, near)
        def _(plane):
            fine.relax(step, plane, inner)
            fine.relax(step, plane + BLOCK + 2 * beside + 9, inner)

    for plane in range(BLOCK):
        u0_ref[plane] = fine.k[0][plane + B_HALO, 8 + BLOCK : 8 + 2 * BLOCK]

    @pl.loop(0, 16)
    def _(index):
        for row in inner:
            first = fine.rest(2 * index + 5, row)
            second = fine.rest(2 * index + 6, row)
            at = pl.ds(pl.multiple_of(32 * index + (row - 16), 8), 8)
            rest_main[at, :] = first[0] + second[0]
            rest_side[at, :] = first[1] + second[1]

    @pl.loop(0, 18)
    def _(index):
        for row in every:
            at = pl.ds(pl.multiple_of(48 * index + (row - 8), 8), 8)
            first, second = 2 * index + 3, 2 * index + 4
            here = slice(row, row + 8)
            sum_main[at, :] = fine.b[0][first, here] + fine.b[0][second, here]
            sum_side[at, :] = fine.b[1][first, here] + fine.b[1][second, here]

    to_main = pair_selector(128, 0, 128, 0, 64)
    to_side = pair_selector(128, 0, 128, 64, 64)
    g_next = split_matmul(halves(rest_main, 256), to_main)
    g_next = 0.5 * (g_next + split_matmul(halves(rest_side, 256), to_side))
    b_next = split_matmul(halves(sum_main, 432), to_main)
    b_next = 0.125 * (b_next + split_matmul(halves(sum_side, 432), to_side))

    middle.clear(20, 24, (1, 18))
    zero = jnp.zeros((8, 128), F32)
    for plane in range(2, 18):
        middle.g[0][plane, 8:16] = zero
        middle.g[0][plane, 24:32] = zero
        middle.g[0][plane, 12:28] = g_next[16 * (plane - 2) : 16 * (plane - 1)]
    for plane in range(1, 19):
        middle.b[0][plane, 8:32] = b_next[24 * (plane - 1) : 24 * plane]
    middle.before(1, 24)

    @pl.loop(2, 18, step=4)
    def _(plane):
        for index in range(4):
            middle.setup(plane + index, 24, index & 1)

    for step in range(3):

        @pl.loop(2, 18, step=4)
        def _(plane):
            for index in range(4):
                middle.relax(step, plane + index, range(8, 32, 8))

    for plane in range(8):
        u1_ref[plane] = middle.k[0][plane + 6, 16:24]
    for index in range(4):
        (first,) = middle.rest(2 * index + 6, 16)
        (second,) = middle.rest(2 * index + 7, 16)
        collect[8 * index : 8 * index + 8] = 0.5 * (first + second)
    for index in range(6):
        first, second = middle.b[0][2 * index + 4, 16:24], middle.b[0][2 * index + 5, 16:24]
        collect[8 * index + 32 : 8 * index + 40] = 0.125 * (first + second)
    collect[80:128] = jnp.zeros((48, 128), F32)
    out = jnp.zeros((16, 128), F32)
    for part in range(4):
        rows = collect[pl.ds(2 * part, 16, stride=8), :]
        rows = rows + collect[pl.ds(2 * part + 1, 16, stride=8), :]
        out = out + split_matmul(rows, pair_selector(128, 0, 128, 32 * part, 32))
    coarse_ref[...] = out


def spread_kernel(low_ref, own_ref, high_ref, out_ref, rows):
    rows[0:4] = low_ref[0:4]
    rows[4:8] = own_ref[0:4]
    rows[8:12] = high_ref[0:4]
    rows[12:17] = low_ref[4:9]
    rows[17:21] = own_ref[5:9]
    rows[21:26] = high_ref[5:10]
    rows[26:32] = jnp.zeros((6, 128), F32)
    value = rows[...]
    for index in range(32):
        out_ref[index] = value


def slab_kernel(gathered_ref, u2_ref, coarse_ref, *scratch):
    slab = Level(scratch[: len(Level.names)], 1, True)
    rest, sums = scratch[len(Level.names) :]
    row = iota((4, 8, 128), 1)
    lane = iota((4, 8, 128), 2)
    group = lane >> 5
    turn = (group - row) & 3

    def exchange(value):
        value = value.reshape(4, 8, 128)
        out = value
        for d in (1, 2, 3):
            moved = pltpu.roll(value, 32 * d, 2)
            near = pltpu.roll(moved, 8 - d, 1)
            far = pltpu.roll(moved, 4 - d, 1)
            out = jnp.where(turn == d, jnp.where(group >= d, near, far), out)
        return out.reshape(32, 128)

    for plane in range(12):
        slab.g[0][plane + 1, 8:40] = exchange(gathered_ref[pl.ds(plane, 32, stride=32), :])
    for plane in range(14):
        slab.b[0][plane, 8:40] = exchange(gathered_ref[pl.ds(plane + 12, 32, stride=32), :])

    slab.clear(14, 32, (0, 13))
    slab.before(0, 32)

    @pl.loop(1, 13, step=4)
    def _(plane):
        for index in range(4):
            slab.setup(plane + index, 32, index & 1)

    for step in range(3):

        @pl.loop(2 + step, 12 - step, step=2)
        def _(plane):
            for index in range(2):
                slab.relax(step, plane + index, range(8, 40, 8))

    for plane in range(4):
        u2_ref[plane] = slab.k[0][plane + 5, 8:40]
    for part in range(2):
        for row in range(8, 40, 8):
            (first,) = slab.rest(5 + 2 * part, row)
            (second,) = slab.rest(6 + 2 * part, row)
            at = slice(32 * part + row - 8, 32 * part + row)
            rest[at] = 0.5 * (first + second)
            here = slice(row, row + 8)
            sums[at] = 0.125 * (slab.b[0][5 + 2 * part, here] + slab.b[0][6 + 2 * part, here])
    g_rows, b_rows = halves(rest, 32), halves(sums, 32)
    value = jnp.zeros((32, 128), F32)
    for part in range(2):
        own = slice(16 * part, 16 * part + 16)
        rows = jnp.concatenate([g_rows[own], b_rows[own]], axis=0)
        value = value + split_matmul(rows, pair_selector(128, 0, 128, 64 * part, 64))
    for index in range(16):
        coarse_ref[index] = value


def coarse_kernel(
    gathered_ref, u0_ref, u1_ref, u2_ref, out_ref,
    r3, rs, k3, ks, inner_3, outer_3, fy3, fz3, d3, ir3, ik3, b3, bs,
    r4, k4, fx4, fy4, fz4, ir4, ik4, g4, b4,
    pair_3, pair_4, twice_3, twice_2, twice_1, twice_0, level_1,
):
    at_x = lax.axis_index("gx")
    at_y = lax.axis_index("gy")
    at_z = lax.axis_index("gz")
    lane = iota((8, 128), 1)
    row8 = iota((8, 128), 0)
    zero = jnp.zeros((8, 128), F32)

    cell = lane & 63
    parity = ((lane >> 6) + row8 + cell) & 1
    first_half = lane < 64
    for ref in (r3, rs, k3, ks, b3, bs):
        for plane in (0, 17):
            ref[plane] = jnp.zeros((32, 128), F32)
    for plane in range(1, 17):
        for ref in (r3, k3, b3, fy3):
            ref[plane, 0:8] = zero
            ref[plane, 24:32] = zero
        for row in (8, 16):
            value = gathered_ref[plane - 1, row + 8 : row + 16]
            b3[plane, row : row + 8] = value
            bs[plane, row : row + 8] = pltpu.roll(value, 64, 1)

    def outer(ref, plane, here):
        return jnp.where(first_half, ref[plane - 1, here], ref[plane + 1, here])

    for plane in range(1, 17):
        for row in (8, 16):
            here = slice(row, row + 8)
            b = b3[plane, here]
            partner, other = bs[plane, here], outer(bs, plane, here)
            y_high = b3[plane, row + 1 : row + 9]
            z_low = jnp.where(cell > 0, pltpu.roll(b, 1, 1), 0.0)
            z_high = jnp.where(cell < 63, pltpu.roll(b, 127, 1), 0.0)
            total = (6.0 * b + (partner + other)) + (
                (b3[plane, row - 1 : row + 7] + y_high) + (z_low + z_high)
            )
            inside = b > 0.0
            inverse = 1.0 / jnp.where(inside, total, 1.0)
            reds = jnp.where(inside & (parity == 0), inverse, 0.0)
            inner_3[plane, here] = b + partner
            outer_3[plane, here] = b + other
            fy3[plane, here] = b + y_high
            fz3[plane, here] = jnp.where(cell < 63, b + z_high, 0.0)
            d3[plane, here] = total
            ir3[plane, here] = reds
            ik3[plane, here] = jnp.where(inside & (parity == 1), inverse, 0.0)
            value = gathered_ref[plane - 1, row - 8 : row] * reds
            r3[plane, here] = value
            rs[plane, here] = pltpu.roll(value, 64, 1)

    def total_3(ref, swapped, plane, row):
        here, low, high = slice(row, row + 8), slice(row - 1, row + 7), slice(row + 1, row + 9)
        v, face = ref[plane, here], fz3[plane, here]
        along_x = inner_3[plane, here] * swapped[plane, here]
        along_x = along_x + outer_3[plane, here] * outer(swapped, plane, here)
        along_y = fy3[plane, here] * ref[plane, high] + fy3[plane, low] * ref[plane, low]
        along_z = face * pltpu.roll(v, 127, 1) + pltpu.roll(face * v, 1, 1)
        return (gathered_ref[plane - 1, row - 8 : row] + along_x) + (along_y + along_z)

    for step in range(3):
        source, inverse, target = (
            ((r3, rs), ik3, (k3, ks)),
            ((k3, ks), ir3, (r3, rs)),
            ((r3, rs), ik3, (k3, ks)),
        )[step]
        for plane in range(1, 17):
            for row in (8, 16):
                here = slice(row, row + 8)
                value = total_3(*source, plane, row) * inverse[plane, here]
                if step == 2:
                    value = value + r3[plane, here]
                target[0][plane, here] = value
                target[1][plane, here] = pltpu.roll(value, 64, 1)

    for plane in range(1, 17):
        for row in (8, 16):
            here = slice(row, row + 8)
            value = total_3(k3, ks, plane, row) - d3[plane, here] * k3[plane, here]
            at = slice(16 * (plane - 1) + row - 8, 16 * (plane - 1) + row)
            pair_3[at] = value + pltpu.roll(value, 64, 1)
            pair_4[at] = b3[plane, here] + bs[plane, here]
    halve = pair_selector(128, 0, 128, 0, 32)
    g4[...] = 0.5 * split_matmul(halves(pair_3, 128), halve).reshape(16, 8, 128)
    b4[0] = zero
    b4[17] = zero
    b4[1:17] = 0.125 * split_matmul(halves(pair_4, 128), halve).reshape(16, 8, 128)

    parity = (row8 + lane) & 1
    for ref in (r4, k4):
        ref[0] = zero
        ref[17] = zero
    fx4[0] = b4[1]
    for plane in range(1, 17):
        b = b4[plane]
        x_high = b4[plane + 1]
        y_low = jnp.where(row8 > 0, pltpu.roll(b, 1, 0), 0.0)
        y_high = jnp.where(row8 < 7, pltpu.roll(b, 7, 0), 0.0)
        z_high = pltpu.roll(b, 127, 1)
        total = (6.0 * b + (b4[plane - 1] + x_high)) + (
            (y_low + y_high) + (pltpu.roll(b, 1, 1) + z_high)
        )
        inside = b > 0.0
        inverse = 1.0 / jnp.where(inside, total, 1.0)
        reds = jnp.where(inside & (parity == (plane - 1) & 1), inverse, 0.0)
        fx4[plane] = b + x_high
        fy4[plane] = jnp.where(row8 < 7, b + y_high, 0.0)
        fz4[plane] = jnp.where(lane < 31, b + z_high, 0.0)
        ir4[plane] = reds
        ik4[plane] = jnp.where(inside & (parity != (plane - 1) & 1), inverse, 0.0)
        r4[plane] = g4[plane - 1] * reds

    def half_4(source, inverse, target):
        for plane in range(1, 17):
            v = source[plane]
            face_y, face_z = fy4[plane], fz4[plane]
            along_x = fx4[plane] * source[plane + 1] + fx4[plane - 1] * source[plane - 1]
            along_y = face_y * pltpu.roll(v, 7, 0) + pltpu.roll(face_y * v, 1, 0)
            along_z = face_z * pltpu.roll(v, 127, 1) + pltpu.roll(face_z * v, 1, 1)
            value = (g4[plane - 1] + along_x) + (along_y + along_z)
            target[plane] = value * inverse[plane]

    half_4(r4, ik4, k4)

    @pl.loop(1, COARSE_SWEEPS)
    def _(sweep):
        half_4(k4, ir4, r4)
        half_4(r4, ik4, k4)

    source = iota((128, 128), 0)
    target = iota((128, 128), 1)
    spread = selector_of((source < 32) & (((target & 63) >> 1) == source))
    value = split_matmul(r4[at_x + 1] + k4[at_x + 1], spread)
    twice_3[pl.ds(0, 8, stride=2), :] = value
    twice_3[pl.ds(1, 8, stride=2), :] = value
    value = k3[at_x + 1, 8:24] + twice_3[...]
    value = pltpu.roll(value, lax.rem(16 - 2 * at_y, 16), 0)
    value = pltpu.roll(value, lax.rem(128 - 16 * at_z, 128), 1)
    level_2 = []
    for part in range(2):
        fine = split_matmul(value, spread_selector(64 * part, 0, 16))[0:8]
        twice_2[pl.ds(0, 8, stride=2), :] = fine
        twice_2[pl.ds(1, 8, stride=2), :] = fine
        for index in range(2):
            own = u2_ref[2 * part + index]
            own = pltpu.roll(own, lax.rem(32 - 4 * at_y, 32), 0)
            own = pltpu.roll(own, lax.rem(128 - 32 * at_z, 128), 1)
            level_2.append(own[0:8] + twice_2[0:8])
    fine = split_matmul(jnp.concatenate(level_2, axis=0), spread_selector(0, 0, 32))
    twice_1[pl.ds(0, 32, stride=2), :] = fine
    twice_1[pl.ds(1, 32, stride=2), :] = fine
    for index in range(8):
        start = 16 * (index // 2)
        level_1[8 * index : 8 * index + 8] = u1_ref[index] + twice_1[start : start + 8]
    fine = split_matmul(level_1[...], spread_selector(0, 0, 64))
    twice_0[pl.ds(0, 64, stride=2), :] = fine
    twice_0[pl.ds(1, 64, stride=2), :] = fine
    for index in range(16):
        start = 16 * (index // 2)
        out_ref[index] = u0_ref[index] + twice_0[start : start + 16]


def call(kernel, megabytes, outs, scratch, *operands):
    whole = pl.BlockSpec(memory_space=pltpu.VMEM)
    return pl.pallas_call(
        kernel,
        out_shape=[jax.ShapeDtypeStruct(shape, F32) for shape in outs],
        in_specs=[whole] * len(operands),
        out_specs=[whole] * len(outs),
        scratch_shapes=[pltpu.VMEM(shape, F32) for shape in scratch],
        compiler_params=pltpu.CompilerParams(vmem_limit_bytes=megabytes << 20),
    )(*operands)


def shift(value, axis, step):
    count = lax.axis_size(axis)
    pairs = [(i, i + step) for i in range(count) if 0 <= i + step < count]
    return lax.ppermute(value, axis, pairs)


def on_device(right_side, conductivity):
    f, b = right_side, conductivity
    upper = jnp.concatenate([f[BLOCK - F_HALO :], b[BLOCK - B_HALO :]], axis=0)
    lower = jnp.concatenate([f[:F_HALO], b[:B_HALO]], axis=0)
    low, high = shift(upper, "gx", 1), shift(lower, "gx", -1)

    strip = (GROUPS, BLOCK, 128)
    main, left, right = call(
        pack_kernel, 4, [(PLANES, BLOCK, 128), strip, strip], [], f, b, low, high
    )
    beyond, before = shift(left, "gz", -1), shift(right, "gz", 1)
    own = jnp.concatenate([main, beyond, before], axis=0)
    low, high = shift(own, "gy", 1), shift(own, "gy", -1)

    u0, u1, coarse = call(
        fine_kernel,
        40,
        [(BLOCK, BLOCK, 128), (8, 8, 128), (16, 128)],
        Level.scratch(2, B_PLANES, ROWS)
        + Level.scratch(1, 20, 24)
        + [(512, 128)] * 2
        + [(864, 128)] * 2
        + [(128, 128)],
        low, own, high,
    )

    low, high = shift(coarse, "gx", 1), shift(coarse, "gx", -1)
    (slab,) = call(spread_kernel, 2, [(32, 32, 128)], [(32, 128)], low, coarse, high)
    slab = lax.all_to_all(slab, ("gy", "gz"), 0, 0, tiled=True)
    u2, coarse = call(
        slab_kernel,
        8,
        [(4, 32, 128), (16, 32, 128)],
        Level.scratch(1, 14, 32) + [(64, 128)] * 2,
        slab.reshape(1024, 128),
    )

    whole = lax.all_to_all(coarse, "gx", 0, 0, tiled=True)
    (out,) = call(
        coarse_kernel,
        8,
        [(BLOCK, BLOCK, 128)],
        [(18, 32, 128)] * 13
        + [(18, 8, 128)] * 7
        + [(16, 8, 128), (18, 8, 128)]
        + [(256, 128)] * 2
        + [(16, 128), (16, 128), (64, 128), (128, 128), (64, 128)],
        whole, u0, u1, u2,
    )
    return out


def solution(mesh):
    spec = P("gx", "gy", "gz")
    return jax.shard_map(
        on_device, mesh=mesh, in_specs=(spec, spec), out_specs=spec, check_vma=False
    )
```

profile of v0, /device:TPU:32, one launch (start us, length us, event | category | flops | bytes accessed | tf_op | source)
XLA Modules:
  0.0 125.9 jit_solution(947515021447321213)
XLA Ops:
  0.0 0.0 copy-start
  0.0 1.0 fusion
  1.0 0.0 copy-done
  1.1 3.8 %collective-permute-start = (f32[25,16,128]{2,1,0:T(8,128)S(1)}, f32[25,16,128]{2,1,0:T(8,128)S(1)}, u32[]{:S(2)}, u32[]{:S(2)}) collective-permute-start(f32[25,16,128]{2,1,0:T(8,128)S(1)} %pad_maximum_fusion), channel_id=1, source_target_pairs={{0,32},{32,64},{64,96},{96,128},{128,160},{160,192},{192,224},{224... | collective-permute-start | bytes 614408 | tf_op jit(solution)/shard_map/ppermute | solution.py:597
  4.9 0.0 copy-start.1
  4.9 5.0 %collective-permute-start.1 = (f32[25,16,128]{2,1,0:T(8,128)S(1)}, f32[25,16,128]{2,1,0:T(8,128)S(1)}, u32[]{:S(2)}, u32[]{:S(2)}) collective-permute-start(f32[25,16,128]{2,1,0:T(8,128)S(1)} %pad_maximum_fusion.1), channel_id=1, source_target_pairs={{32,0},{64,32},{96,64},{128,96},{160,128},{192,160},{224,192},{256... | collective-permute-start | bytes 614408 | tf_op jit(solution)/shard_map/ppermute | solution.py:597
  9.9 1.6 %collective-permute-done.low_ref = f32[25,16,128]{2,1,0:T(8,128)S(1)} collective-permute-done((f32[25,16,128]{2,1,0:T(8,128)S(1)}, f32[25,16,128]{2,1,0:T(8,128)S(1)}, u32[]{:S(2)}, u32[]{:S(2)}) %collective-permute-start) | collective-permute-done | bytes 204832 | tf_op jit(solution)/shard_map/ppermute | solution.py:597
  11.5 2.1 %collective-permute-done.1.high_ref = f32[25,16,128]{2,1,0:T(8,128)S(1)} collective-permute-done((f32[25,16,128]{2,1,0:T(8,128)S(1)}, f32[25,16,128]{2,1,0:T(8,128)S(1)}, u32[]{:S(2)}, u32[]{:S(2)}) %collective-permute-start.1) | collective-permute-done | bytes 204832 | tf_op jit(solution)/shard_map/ppermute | solution.py:597
  13.7 0.0 copy-done.1
  13.7 0.2 shard_map.28
  13.9 1.3 %collective-permute-start.2 = (f32[11,16,128]{2,1,0:T(8,128)S(1)}, f32[11,16,128]{2,1,0:T(8,128)S(1)}, u32[]{:S(2)}, u32[]{:S(2)}) collective-permute-start(f32[11,16,128]{2,1,0:T(8,128)S(1)} %get-tuple-element.14), channel_id=1, source_target_pairs={{1,0},{2,1},{3,2},{5,4},{6,5},{7,6},{9,8},{10,9},{11,10},{13,12},{... | collective-permute-start | bytes 270344 | tf_op jit(solution)/shard_map/ppermute | solution.py:597
  15.2 4.6 %collective-permute-start.3 = (f32[11,16,128]{2,1,0:T(8,128)S(1)}, f32[11,16,128]{2,1,0:T(8,128)S(1)}, u32[]{:S(2)}, u32[]{:S(2)}) collective-permute-start(f32[11,16,128]{2,1,0:T(8,128)S(1)} %get-tuple-element.15), channel_id=1, source_target_pairs={{0,1},{1,2},{2,3},{4,5},{5,6},{6,7},{8,9},{9,10},{10,11},{12,13},{... | collective-permute-start | bytes 270344 | tf_op jit(solution)/shard_map/ppermute | solution.py:597
  19.8 0.5 collective-permute-done.2
  20.3 1.5 %collective-permute-done.3 = f32[11,16,128]{2,1,0:T(8,128)S(1)} collective-permute-done((f32[11,16,128]{2,1,0:T(8,128)S(1)}, f32[11,16,128]{2,1,0:T(8,128)S(1)}, u32[]{:S(2)}, u32[]{:S(2)}) %collective-permute-start.3) | collective-permute-done | bytes 90144 | tf_op jit(solution)/shard_map/ppermute | solution.py:597
  21.9 1.3 %collective-permute-start.5 = (f32[104,16,128]{2,1,0:T(8,128)S(1)}, f32[104,16,128]{2,1,0:T(8,128)S(1)}, u32[]{:S(2)}, u32[]{:S(2)}) collective-permute-start(f32[104,16,128]{2,1,0:T(8,128)S(1)} %constant_dynamic-update-slice_fusion.own_ref), channel_id=1, source_target_pairs={{4,0},{8,4},{12,8},{16,12},{20,16},{24,20},{28,24},{5,1},{9,5},{13... | collective-permute-start | bytes 2555912 | tf_op jit(solution)/shard_map/ppermute | solution.py:597
  23.2 3.1 %collective-permute-start.4 = (f32[104,16,128]{2,1,0:T(8,128)S(1)}, f32[104,16,128]{2,1,0:T(8,128)S(1)}, u32[]{:S(2)}, u32[]{:S(2)}) collective-permute-start(f32[104,16,128]{2,1,0:T(8,128)S(1)} %constant_dynamic-update-slice_fusion.own_ref), channel_id=1, source_target_pairs={{0,4},{4,8},{8,12},{12,16},{16,20},{20,24},{24,28},{1,5},{5,9},{9,... | collective-permute-start | bytes 2555912 | tf_op jit(solution)/shard_map/ppermute | solution.py:597
  26.3 0.0 collective-permute-done.5.high_ref
  26.3 1.9 %collective-permute-done.4.low_ref = f32[104,16,128]{2,1,0:T(8,128)S(1)} collective-permute-done((f32[104,16,128]{2,1,0:T(8,128)S(1)}, f32[104,16,128]{2,1,0:T(8,128)S(1)}, u32[]{:S(2)}, u32[]{:S(2)}) %collective-permute-start.4) | collective-permute-done | bytes 852000 | tf_op jit(solution)/shard_map/ppermute | solution.py:597
  28.2 17.0 %shard_map.29 = (f32[16,16,128]{2,1,0:T(8,128)S(1)}, f32[8,8,128]{2,1,0:T(8,128)S(1)}, f32[16,128]{1,0:T(8,128)S(1)}) custom-call(f32[104,16,128]{2,1,0:T(8,128)S(1)} %collective-permute-done.4.low_ref, f32[104,16,128]{2,1,0:T(8,128)S(1)} %constant_dynamic-update-slice_fusion.own_ref, f32[104,16,128]{2,1,0:T(8,128)S(1)} %collective-permute-done.5.high_ref), custom_call_target="tpu_custom_call" | custom-call | tf_op jit(solution)/shard_map/pallas_call | solution.py:584
  45.2 3.9 %collective-permute-start.7 = (f32[16,128]{1,0:T(8,128)S(1)}, f32[16,128]{1,0:T(8,128)S(1)}, u32[]{:S(2)}, u32[]{:S(2)}) collective-permute-start(f32[16,128]{1,0:T(8,128)S(1)} %get-tuple-element.16.own_ref), channel_id=1, source_target_pairs={{32,0},{64,32},{96,64},{128,96},{160,128},{192,160},{224,192},{256... | collective-permute-start | bytes 24584 | tf_op jit(solution)/shard_map/ppermute | solution.py:597
  49.1 3.1 %collective-permute-start.6 = (f32[16,128]{1,0:T(8,128)S(1)}, f32[16,128]{1,0:T(8,128)S(1)}, u32[]{:S(2)}, u32[]{:S(2)}) collective-permute-start(f32[16,128]{1,0:T(8,128)S(1)} %get-tuple-element.16.own_ref), channel_id=1, source_target_pairs={{0,32},{32,64},{64,96},{96,128},{128,160},{160,192},{192,224},{224... | collective-permute-start | bytes 24584 | tf_op jit(solution)/shard_map/ppermute | solution.py:597
  52.2 0.0 collective-permute-done.7.high_ref
  52.2 2.4 %collective-permute-done.6.low_ref = f32[16,128]{1,0:T(8,128)S(1)} collective-permute-done((f32[16,128]{1,0:T(8,128)S(1)}, f32[16,128]{1,0:T(8,128)S(1)}, u32[]{:S(2)}, u32[]{:S(2)}) %collective-permute-start.6) | collective-permute-done | bytes 8224 | tf_op jit(solution)/shard_map/ppermute | solution.py:597
  54.7 28.2 %all_to_all.10 = f32[32,32,128]{2,1,0:T(8,128)S(1)} all-to-all(f32[32,32,128]{2,1,0:T(8,128)S(1)} %shard_map.30), channel_id=1, replica_groups=mesh['gx'=16,'gy'=8,'gz'=4] {'gy','gz'}, dimensions={0} | all-to-all | bytes 1048576 | tf_op jit(solution)/shard_map/all_to_all | solution.py:628
  82.9 2.4 %shard_map.31 = (f32[4,32,128]{2,1,0:T(8,128)S(1)}, f32[16,32,128]{2,1,0:T(8,128)S(1)}) custom-call(f32[1024,128]{1,0:T(8,128)S(1)} %bitcast.1), custom_call_target="tpu_custom_call" | custom-call | tf_op jit(solution)/shard_map/pallas_call | solution.py:584
  85.3 36.0 %all_to_all.11.gathered_ref = f32[16,32,128]{2,1,0:T(8,128)S(1)} all-to-all(f32[16,32,128]{2,1,0:T(8,128)S(1)} %get-tuple-element.17), channel_id=1, replica_groups=mesh['gx'=16,'gy'=8,'gz'=4] {'gx'}, dimensions={0} | all-to-all | bytes 524288 | tf_op jit(solution)/shard_map/all_to_all | solution.py:637
  121.3 4.5 %shard_map.32 = f32[16,16,128]{2,1,0:T(8,128)} custom-call(f32[16,32,128]{2,1,0:T(8,128)S(1)} %all_to_all.11.gathered_ref, f32[16,16,128]{2,1,0:T(8,128)S(1)} %get-tuple-element.18.u0_ref, f32[8,8,128]{2,1,0:T(8,128)S(1)} %get-tuple-element.19.u1_ref, f32[4,32,128]{2,1,0:T(8,128)S(1)} %get-tuple-element.20.u2_ref), custom_call_target="tpu_custom_call" | custom-call | tf_op jit(solution)/shard_map/pallas_call | solution.py:584
  (7 shorter events, 0.2 us)
Async XLA Ops:
  0.0 1.0 copy-start
  1.1 10.5 %collective-permute-start = (f32[25,16,128]{2,1,0:T(8,128)S(1)}, f32[25,16,128]{2,1,0:T(8,128)S(1)}, u32[]{:S(2)}, u32[]{:S(2)}) collective-permute-start(f32[25,16,128]{2,1,0:T(8,128)S(1)} %pad_maximum_fusion), channel_id=1, source_target_pairs={{0,32},{32,64},{64,96},{96,128},{128,160},{160,192},{192,224},{224... | collective-permute-start | bytes 614408 | tf_op jit(solution)/shard_map/ppermute | solution.py:597
  4.9 8.8 %copy-start.1 = (f32[16,16,128]{2,1,0:T(8,128)S(1)}, f32[16,16,128]{2,1,0:T(8,128)}, u32[]{:S(2)}) copy-start(f32[16,16,128]{2,1,0:T(8,128)} %f_ref.1) | copy-start | bytes 393220
  4.9 8.7 %collective-permute-start.1 = (f32[25,16,128]{2,1,0:T(8,128)S(1)}, f32[25,16,128]{2,1,0:T(8,128)S(1)}, u32[]{:S(2)}, u32[]{:S(2)}) collective-permute-start(f32[25,16,128]{2,1,0:T(8,128)S(1)} %pad_maximum_fusion.1), channel_id=1, source_target_pairs={{32,0},{64,32},{96,64},{128,96},{160,128},{192,160},{224,192},{256... | collective-permute-start | bytes 614408 | tf_op jit(solution)/shard_map/ppermute | solution.py:597
  13.9 6.4 %collective-permute-start.2 = (f32[11,16,128]{2,1,0:T(8,128)S(1)}, f32[11,16,128]{2,1,0:T(8,128)S(1)}, u32[]{:S(2)}, u32[]{:S(2)}) collective-permute-start(f32[11,16,128]{2,1,0:T(8,128)S(1)} %get-tuple-element.14), channel_id=1, source_target_pairs={{1,0},{2,1},{3,2},{5,4},{6,5},{7,6},{9,8},{10,9},{11,10},{13,12},{... | collective-permute-start | bytes 270344 | tf_op jit(solution)/shard_map/ppermute | solution.py:597
  15.2 6.7 %collective-permute-start.3 = (f32[11,16,128]{2,1,0:T(8,128)S(1)}, f32[11,16,128]{2,1,0:T(8,128)S(1)}, u32[]{:S(2)}, u32[]{:S(2)}) collective-permute-start(f32[11,16,128]{2,1,0:T(8,128)S(1)} %get-tuple-element.15), channel_id=1, source_target_pairs={{0,1},{1,2},{2,3},{4,5},{5,6},{6,7},{8,9},{9,10},{10,11},{12,13},{... | collective-permute-start | bytes 270344 | tf_op jit(solution)/shard_map/ppermute | solution.py:597
  21.9 4.4 %collective-permute-start.5 = (f32[104,16,128]{2,1,0:T(8,128)S(1)}, f32[104,16,128]{2,1,0:T(8,128)S(1)}, u32[]{:S(2)}, u32[]{:S(2)}) collective-permute-start(f32[104,16,128]{2,1,0:T(8,128)S(1)} %constant_dynamic-update-slice_fusion.own_ref), channel_id=1, source_target_pairs={{4,0},{8,4},{12,8},{16,12},{20,16},{24,20},{28,24},{5,1},{9,5},{13... | collective-permute-start | bytes 2555912 | tf_op jit(solution)/shard_map/ppermute | solution.py:597
  23.2 5.0 %collective-permute-start.4 = (f32[104,16,128]{2,1,0:T(8,128)S(1)}, f32[104,16,128]{2,1,0:T(8,128)S(1)}, u32[]{:S(2)}, u32[]{:S(2)}) collective-permute-start(f32[104,16,128]{2,1,0:T(8,128)S(1)} %constant_dynamic-update-slice_fusion.own_ref), channel_id=1, source_target_pairs={{0,4},{4,8},{8,12},{12,16},{16,20},{20,24},{24,28},{1,5},{5,9},{9,... | collective-permute-start | bytes 2555912 | tf_op jit(solution)/shard_map/ppermute | solution.py:597
  45.2 7.0 %collective-permute-start.7 = (f32[16,128]{1,0:T(8,128)S(1)}, f32[16,128]{1,0:T(8,128)S(1)}, u32[]{:S(2)}, u32[]{:S(2)}) collective-permute-start(f32[16,128]{1,0:T(8,128)S(1)} %get-tuple-element.16.own_ref), channel_id=1, source_target_pairs={{32,0},{64,32},{96,64},{128,96},{160,128},{192,160},{224,192},{256... | collective-permute-start | bytes 24584 | tf_op jit(solution)/shard_map/ppermute | solution.py:597
  49.1 5.5 %collective-permute-start.6 = (f32[16,128]{1,0:T(8,128)S(1)}, f32[16,128]{1,0:T(8,128)S(1)}, u32[]{:S(2)}, u32[]{:S(2)}) collective-permute-start(f32[16,128]{1,0:T(8,128)S(1)} %get-tuple-element.16.own_ref), channel_id=1, source_target_pairs={{0,32},{32,64},{64,96},{96,128},{128,160},{160,192},{192,224},{224... | collective-permute-start | bytes 24584 | tf_op jit(solution)/shard_map/ppermute | solution.py:597
where the time goes:
time: 126 us
  blocking collectives  64.2 us (51%)
  starting transfers between devices  26 us (21%)
  Pallas kernels  24.2 us (19%)
  waiting for transfers between devices  10.2 us (8%)
    all_to_all x1, blocking collectives, on_device(): whole = lax.all_to_all(coarse, 'gx', 0, 0, tiled=True)  36 us
    all_to_all x1, blocking collectives, on_device(): slab = lax.all_to_all(slab, ('gy', 'gz'), 0, 0, tiled=True)  28.2 us
    ppermute x8, starting transfers between devices, shift(): return lax.ppermute(value, axis, pairs)  26 us
    pallas_call x5, Pallas kernels, call(): pl.pallas_call(kernel, out_shape=[jax.ShapeDtypeStruct(shape, F32) for sh...  24.2 us
    ppermute x8, waiting for transfers between devices, shift(): return lax.ppermute(value, axis, pairs)  10.2 us
  transfers between devices with their start and end apart: 8, of which 6 were waited for; matrix products, arithmetic and copies ran while one was open for 0% of the time, Pallas kernels for 0%

commit v1 on v0

--- a/solution.py
+++ b/solution.py
@@ -14,6 +14,24 @@
 GROUPS = -(-PLANES // 8)
 F_GROUPS = F_PLANES // 8
 ROWS = 48
+
+
+def rows_of(index):
+    if index < F_PLANES:
+        return F_HALO - max(F_HALO - index, index - F_HALO - BLOCK + 1, 0)
+    index -= F_PLANES
+    return B_HALO - max(B_HALO - index, index - B_HALO - BLOCK + 1, 0)
+
+
+COUNTS = [rows_of(index) for index in range(PLANES)]
+OFFSETS = [sum(COUNTS[:index]) for index in range(PLANES)]
+PACKED = sum(COUNTS)
+STRIP_ROWS = [
+    8 * -(-max(0, max(COUNTS[8 * group : 8 * group + 8]) - 1) // 8) for group in range(GROUPS)
+]
+STRIP_OFFSETS = [PACKED + sum(STRIP_ROWS[:group]) for group in range(GROUPS)]
+SIDE = sum(STRIP_ROWS)
+PAYLOAD = PACKED + 2 * SIDE
 COARSE_SWEEPS = 8
 F32 = jnp.float32
 
@@ -80,13 +98,15 @@
 
     def clear(self, planes, rows, ends):
         zero = jnp.zeros((8, 128), F32)
-        for refs in (self.b, self.fy, self.r, self.k):
-            for ref in refs:
-
-                @pl.loop(0, planes)
-                def _(plane):
+
+        @pl.loop(0, planes)
+        def _(plane):
+            for refs in (self.b, self.r, self.k):
+                for ref in refs:
                     ref[plane, 0:8] = zero
                     ref[plane, rows + 8 : rows + 16] = zero
+            for ref in self.fy:
+                ref[plane, 0:8] = zero
 
         for refs in (self.r, self.k):
             for ref in refs:
@@ -129,44 +149,50 @@
                 self.r[column][here] = g[column] * reds
                 self.k[column][here] = jnp.zeros((8, 128), F32)
 
-    def total(self, source, plane, row):
-        v = self.at(source, plane, row)
-        face_z = self.at(self.fz, plane, row)
+    def total(self, source, base, step, row, held=None):
+        held = {} if held is None else held
+
+        def load(ref, plane):
+            key = (id(ref), plane)
+            if key not in held:
+                held[key] = ref[base + plane, row : row + 8]
+            return held[key]
+
+        v = [load(ref, step) for ref in source]
+        face_z = [load(ref, step) for ref in self.fz]
         z_high = self.turn(v, 1)
         z_low = self.turn([face * value for face, value in zip(face_z, v)], -1)
         out = []
         for column in range(self.columns):
             ref, fx, fy = source[column], self.fx[column], self.fy[column]
-            here = slice(row, row + 8)
-            along_x = (
-                fx[plane, here] * ref[plane + 1, here]
-                + fx[plane - 1, here] * ref[plane - 1, here]
-            )
+            along_x = load(fx, step) * load(ref, step + 1) + load(fx, step - 1) * load(ref, step - 1)
             low, high = slice(row - 1, row + 7), slice(row + 1, row + 9)
-            along_y = fy[plane, here] * ref[plane, high] + fy[plane, low] * ref[plane, low]
+            plane = base + step
+            along_y = load(fy, step) * ref[plane, high] + fy[plane, low] * ref[plane, low]
             along_z = face_z[column] * z_high[column] + z_low[column]
-            out.append((self.g[column][plane, here] + along_x) + (along_y + along_z))
+            out.append((load(self.g[column], step) + along_x) + (along_y + along_z))
         return out
 
-    def relax(self, step, plane, rows):
+    def relax(self, step, base, count, rows):
         source, inverse, target = (
             (self.r, self.ik, self.k),
             (self.k, self.ir, self.r),
             (self.r, self.ik, self.k),
         )[step]
-        results = []
         for row in rows:
-            values = self.total(source, plane, row)
-            scale = self.at(inverse, plane, row)
-            values = [value * factor for value, factor in zip(values, scale)]
-            if step == 2:
-                values = [a + b for a, b in zip(values, self.at(self.r, plane, row))]
-            results.append(values)
-        for row, values in zip(rows, results):
-            self.put(target, plane, row, values)
-
-    def rest(self, plane, row):
-        values = self.total(self.k, plane, row)
+            held = {}
+            for index in range(count):
+                values = self.total(source, base, index, row, held)
+                scale = self.at(inverse, base + index, row)
+                values = [value * factor for value, factor in zip(values, scale)]
+                if step == 2:
+                    own = self.at(self.r, base + index, row)
+                    values = [a + b for a, b in zip(values, own)]
+                self.put(target, base + index, row, values)
+
+    def rest(self, base, row, step=0, held=None):
+        values = self.total(self.k, base, step, row, held)
+        plane = base + step
         out = []
         for column, value in enumerate(values):
             here = (plane, slice(row, row + 8))
@@ -179,7 +205,9 @@
     return ref[pl.ds(0, rows, stride=2), :] + ref[pl.ds(1, rows, stride=2), :]
 
 
-def pack_kernel(f_ref, b_ref, low_ref, high_ref, main_ref, left_ref, right_ref):
+def pack_kernel(
+    f_ref, b_ref, low_ref, high_ref, main_ref, left_ref, right_ref, down_ref, up_ref
+):
     lane = iota((BLOCK, 128), 1)
 
     def source(index):
@@ -205,6 +233,10 @@
                 break
             plane = source(index)
             main_ref[index] = plane
+            count, start = COUNTS[index], OFFSETS[index]
+            if count:
+                down_ref[start : start + count] = plane[0:count]
+                up_ref[start : start + count] = plane[BLOCK - count : BLOCK]
             turned = pltpu.roll(plane, 16 * slot, 1) if slot else plane
             left = jnp.where((lane >> 4) == slot, turned, left)
             right = jnp.where((lane >> 4) == ((slot - 1) & 7), turned, right)
@@ -212,50 +244,76 @@
         right_ref[group] = right
 
 
-def fine_kernel(low_ref, own_ref, high_ref, u0_ref, u1_ref, coarse_ref, *scratch):
+def join_kernel(down_ref, up_ref, after_ref, before_ref, down_out, up_out):
+    down_out[0:PACKED] = down_ref[...]
+    up_out[0:PACKED] = up_ref[...]
+    for side, strips in enumerate((after_ref, before_ref)):
+        for group in range(GROUPS):
+            count = STRIP_ROWS[group]
+            start = STRIP_OFFSETS[group] + side * SIDE
+            if count:
+                down_out[start : start + count] = strips[group, 0:count]
+                up_out[start : start + count] = strips[group, BLOCK - count : BLOCK]
+
+
+def fine_kernel(
+    low_ref, high_ref, main_ref, after_ref, before_ref, u0_ref, u1_ref, coarse_ref, *scratch
+):
     count = len(Level.names)
     fine = Level(scratch[: 2 * count], 2, False)
     middle = Level(scratch[2 * count : 3 * count], 1, False)
     rest_main, rest_side, sum_main, sum_side, collect = scratch[3 * count :]
 
-    lane = iota((BLOCK, 128), 1)
-    even = ((lane >> 4) & 1) == 0
-    edges = (lane < 16) | (lane >= 112)
-
-    def place(target, first, group, slots, scale):
-        for part, source in enumerate((low_ref, own_ref, high_ref)):
-            after, before = source[PLANES + group], source[PLANES + GROUPS + group]
-            merged = (jnp.where(even, after, before), jnp.where(even, before, after))
-            rows = slice(8 + BLOCK * part, 8 + BLOCK * part + BLOCK)
-            for slot in slots:
-                side = merged[slot & 1]
-                if slot:
-                    side = pltpu.roll(side, 128 - 16 * slot, 1)
-                side = jnp.where(edges, side, 0.0)
-                plane = source[group * 8 + slot]
-                if scale != 1.0:
-                    side, plane = side * scale, plane * scale
-                target[0][first + slot, rows] = plane
-                target[1][first + slot, rows] = side
-
-    @pl.loop(0, F_GROUPS)
-    def _(group):
-        place(fine.g, group * 8 + 1, group, range(8), 2.0)
-
-    @pl.loop(F_GROUPS, GROUPS - 1)
-    def _(group):
-        place(fine.b, group * 8 - F_PLANES, group, range(8), 1.0)
-
-    group = GROUPS - 1
-    place(fine.b, group * 8 - F_PLANES, group, range(PLANES - 8 * group), 1.0)
+    blank = jnp.zeros((BLOCK, 128), F32)
+
+    def unpack(after, before):
+        even = ((iota(after.shape, 1) >> 4) & 1) == 0
+        return jnp.where(even, after, before), jnp.where(even, before, after)
+
+    def place(target, plane, index, scale):
+        group, slot = index // 8, index % 8
+        count, start = COUNTS[index], OFFSETS[index]
+        main, side = target
+        first, own, last = 8, 8 + BLOCK, 8 + 2 * BLOCK
+        main[plane, first:own] = blank
+        main[plane, last : last + BLOCK] = blank
+        main[plane, own:last] = main_ref[index] * scale
+        if count:
+            main[plane, own - count : own] = low_ref[start : start + count] * scale
+            main[plane, last : last + count] = high_ref[start : start + count] * scale
+
+        def turned(pair):
+            value = pair[slot & 1]
+            if slot:
+                value = pltpu.roll(value, 128 - 16 * slot, 1)
+            lane = iota(value.shape, 1)
+            return jnp.where((lane < 16) | (lane >= 112), value, 0.0) * scale
+
+        side[plane, own:last] = turned(unpack(after_ref[group], before_ref[group]))
+        rows = STRIP_ROWS[group]
+        if rows < BLOCK:
+            side[plane, first:own] = blank
+            side[plane, last : last + BLOCK] = blank
+        if rows:
+            start = STRIP_OFFSETS[group]
+            beyond = slice(start, start + rows), slice(start + SIDE, start + SIDE + rows)
+            side[plane, own - rows : own] = turned(unpack(low_ref[beyond[0]], low_ref[beyond[1]]))
+            side[plane, last : last + rows] = turned(
+                unpack(high_ref[beyond[0]], high_ref[beyond[1]])
+            )
+
+    for index in range(F_PLANES):
+        place(fine.g, index + 1, index, 2.0)
+    for index in range(F_PLANES, PLANES):
+        place(fine.b, index - F_PLANES, index, 1.0)
 
     fine.clear(B_PLANES, ROWS, (0, B_PLANES - 1))
     fine.before(0, ROWS)
 
-    @pl.loop(1, B_PLANES - 1, step=2)
+    @pl.loop(1, B_PLANES - 1, step=4)
     def _(plane):
-        fine.setup(plane, ROWS, 0)
-        fine.setup(plane + 1, ROWS, 1)
+        for index in range(4):
+            fine.setup(plane + index, ROWS, index & 1)
 
     every = range(8, ROWS + 8, 8)
     inner = range(16, ROWS, 8)
@@ -263,15 +321,16 @@
         beside = 2 - step
         near = B_HALO - beside
 
-        @pl.loop(near, near + BLOCK + 2 * beside, step=2)
+        count = (4, 3, 4)[step]
+
+        @pl.loop(near, near + BLOCK + 2 * beside, step=count)
         def _(plane):
-            fine.relax(step, plane, every)
-            fine.relax(step, plane + 1, every)
-
-        @pl.loop(near - 9, near)
+            fine.relax(step, plane, count, every)
+
+        @pl.loop(near - 9, near, step=3)
         def _(plane):
-            fine.relax(step, plane, inner)
-            fine.relax(step, plane + BLOCK + 2 * beside + 9, inner)
+            fine.relax(step, plane, 3, inner)
+            fine.relax(step, plane + BLOCK + 2 * beside + 9, 3, inner)
 
     for plane in range(BLOCK):
         u0_ref[plane] = fine.k[0][plane + B_HALO, 8 + BLOCK : 8 + 2 * BLOCK]
@@ -279,8 +338,9 @@
     @pl.loop(0, 16)
     def _(index):
         for row in inner:
-            first = fine.rest(2 * index + 5, row)
-            second = fine.rest(2 * index + 6, row)
+            held = {}
+            first = fine.rest(2 * index + 5, row, 0, held)
+            second = fine.rest(2 * index + 5, row, 1, held)
             at = pl.ds(pl.multiple_of(32 * index + (row - 16), 8), 8)
             rest_main[at, :] = first[0] + second[0]
             rest_side[at, :] = first[1] + second[1]
@@ -320,8 +380,7 @@
 
         @pl.loop(2, 18, step=4)
         def _(plane):
-            for index in range(4):
-                middle.relax(step, plane + index, range(8, 32, 8))
+            middle.relax(step, plane, 4, range(8, 32, 8))
 
     for plane in range(8):
         u1_ref[plane] = middle.k[0][plane + 6, 16:24]
@@ -389,8 +448,7 @@
 
         @pl.loop(2 + step, 12 - step, step=2)
         def _(plane):
-            for index in range(2):
-                slab.relax(step, plane + index, range(8, 40, 8))
+            slab.relax(step, plane, 2, range(8, 40, 8))
 
     for plane in range(4):
         u2_ref[plane] = slab.k[0][plane + 5, 8:40]
@@ -604,12 +662,13 @@
     low, high = shift(upper, "gx", 1), shift(lower, "gx", -1)
 
     strip = (GROUPS, BLOCK, 128)
-    main, left, right = call(
-        pack_kernel, 4, [(PLANES, BLOCK, 128), strip, strip], [], f, b, low, high
+    packed = (PACKED, 128)
+    main, left, right, down, up = call(
+        pack_kernel, 4, [(PLANES, BLOCK, 128), strip, strip, packed, packed], [], f, b, low, high
     )
-    beyond, before = shift(left, "gz", -1), shift(right, "gz", 1)
-    own = jnp.concatenate([main, beyond, before], axis=0)
-    low, high = shift(own, "gy", 1), shift(own, "gy", -1)
+    after, before = shift(left, "gz", -1), shift(right, "gz", 1)
+    down, up = call(join_kernel, 4, [(PAYLOAD, 128)] * 2, [], down, up, after, before)
+    low, high = shift(up, "gy", 1), shift(down, "gy", -1)
 
     u0, u1, coarse = call(
         fine_kernel,
@@ -620,7 +679,7 @@
         + [(512, 128)] * 2
         + [(864, 128)] * 2
         + [(128, 128)],
-        low, own, high,
+        low, high, main, after, before,
     )
 
     low, high = shift(coarse, "gx", 1), shift(coarse, "gx", -1)

time: 126 us -> 117 us (0.929)
  Pallas kernels: 24.2 us -> 19.4 us
  blocking collectives: 64.2 us -> 60.7 us
  starting transfers between devices: 26 us -> 24.2 us
    pallas_call x5 -> x6, Pallas kernels: 24.2 us -> 19.4 us  [call(): pl.pallas_call(kernel, out_shape=[jax.ShapeDtypeStruct(shape, F32) for sh...]
    all_to_all x1, blocking collectives: 28.2 us -> 24.9 us  [on_device(): slab = lax.all_to_all(slab, ('gy', 'gz'), 0, 0, tiled=True)]
    ppermute x8, starting transfers between devices: 26 us -> 24.2 us  [shift(): return lax.ppermute(value, axis, pairs)]
  transfers between devices with their start and end apart: 8 -> 8, of which waited for: 6 -> 7; matrix products, arithmetic and copies ran while one was open for 0% -> 0% of each run, Pallas kernels for 0% -> 0%
where the time goes in v1:
time: 117 us
  blocking collectives  60.7 us (52%)
  starting transfers between devices  24.2 us (21%)
  Pallas kernels  19.4 us (17%)
  waiting for transfers between devices  11.4 us (10%)
    all_to_all x1, blocking collectives, on_device(): whole = lax.all_to_all(coarse, 'gx', 0, 0, tiled=True)  35.7 us
    all_to_all x1, blocking collectives, on_device(): slab = lax.all_to_all(slab, ('gy', 'gz'), 0, 0, tiled=True)  24.9 us
    ppermute x8, starting transfers between devices, shift(): return lax.ppermute(value, axis, pairs)  24.2 us
    pallas_call x6, Pallas kernels, call(): pl.pallas_call(kernel, out_shape=[jax.ShapeDtypeStruct(shape, F32) for sh...  19.4 us
    ppermute x8, waiting for transfers between devices, shift(): return lax.ppermute(value, axis, pairs)  11.4 us
  transfers between devices with their start and end apart: 8, of which 7 were waited for; matrix products, arithmetic and copies ran while one was open for 0% of the time, Pallas kernels for 0%

profile of v1, /device:TPU:32, one launch (start us, length us, event | category | flops | bytes accessed | tf_op | source)
XLA Modules:
  0.0 116.9 jit_solution(17253156655180977612)
XLA Ops:
  0.0 0.0 copy-start
  0.0 1.0 fusion
  1.0 0.0 copy-done
  1.1 3.8 %collective-permute-start = (f32[25,16,128]{2,1,0:T(8,128)S(1)}, f32[25,16,128]{2,1,0:T(8,128)S(1)}, u32[]{:S(2)}, u32[]{:S(2)}) collective-permute-start(f32[25,16,128]{2,1,0:T(8,128)S(1)} %pad_maximum_fusion), channel_id=1, source_target_pairs={{0,32},{32,64},{64,96},{96,128},{128,160},{160,192},{192,224},{224... | collective-permute-start | bytes 614408 | tf_op jit(solution)/shard_map/ppermute | solution.py:655
  4.9 0.0 copy-start.1
  4.9 5.0 %collective-permute-start.1 = (f32[25,16,128]{2,1,0:T(8,128)S(1)}, f32[25,16,128]{2,1,0:T(8,128)S(1)}, u32[]{:S(2)}, u32[]{:S(2)}) collective-permute-start(f32[25,16,128]{2,1,0:T(8,128)S(1)} %pad_maximum_fusion.1), channel_id=1, source_target_pairs={{32,0},{64,32},{96,64},{128,96},{160,128},{192,160},{224,192},{256... | collective-permute-start | bytes 614408 | tf_op jit(solution)/shard_map/ppermute | solution.py:655
  9.9 1.6 %collective-permute-done.low_ref = f32[25,16,128]{2,1,0:T(8,128)S(1)} collective-permute-done((f32[25,16,128]{2,1,0:T(8,128)S(1)}, f32[25,16,128]{2,1,0:T(8,128)S(1)}, u32[]{:S(2)}, u32[]{:S(2)}) %collective-permute-start) | collective-permute-done | bytes 204832 | tf_op jit(solution)/shard_map/ppermute | solution.py:655
  11.5 2.1 %collective-permute-done.1.high_ref = f32[25,16,128]{2,1,0:T(8,128)S(1)} collective-permute-done((f32[25,16,128]{2,1,0:T(8,128)S(1)}, f32[25,16,128]{2,1,0:T(8,128)S(1)}, u32[]{:S(2)}, u32[]{:S(2)}) %collective-permute-start.1) | collective-permute-done | bytes 204832 | tf_op jit(solution)/shard_map/ppermute | solution.py:655
  13.7 0.0 copy-done.1
  13.7 0.2 shard_map.28
  13.9 1.3 %collective-permute-start.2 = (f32[11,16,128]{2,1,0:T(8,128)S(1)}, f32[11,16,128]{2,1,0:T(8,128)S(1)}, u32[]{:S(2)}, u32[]{:S(2)}) collective-permute-start(f32[11,16,128]{2,1,0:T(8,128)S(1)} %get-tuple-element.19), channel_id=1, source_target_pairs={{1,0},{2,1},{3,2},{5,4},{6,5},{7,6},{9,8},{10,9},{11,10},{13,12},{... | collective-permute-start | bytes 270344 | tf_op jit(solution)/shard_map/ppermute | solution.py:655
  15.2 4.6 %collective-permute-start.3 = (f32[11,16,128]{2,1,0:T(8,128)S(1)}, f32[11,16,128]{2,1,0:T(8,128)S(1)}, u32[]{:S(2)}, u32[]{:S(2)}) collective-permute-start(f32[11,16,128]{2,1,0:T(8,128)S(1)} %get-tuple-element.20), channel_id=1, source_target_pairs={{0,1},{1,2},{2,3},{4,5},{5,6},{6,7},{8,9},{9,10},{10,11},{12,13},{... | collective-permute-start | bytes 270344 | tf_op jit(solution)/shard_map/ppermute | solution.py:655
  19.8 0.6 collective-permute-done.2.after_ref
  20.3 1.6 %collective-permute-done.3.before_ref = f32[11,16,128]{2,1,0:T(8,128)S(1)} collective-permute-done((f32[11,16,128]{2,1,0:T(8,128)S(1)}, f32[11,16,128]{2,1,0:T(8,128)S(1)}, u32[]{:S(2)}, u32[]{:S(2)}) %collective-permute-start.3) | collective-permute-done | bytes 90144 | tf_op jit(solution)/shard_map/ppermute | solution.py:655
  21.9 0.1 shard_map.29
  22.0 1.3 %collective-permute-start.4 = (f32[944,128]{1,0:T(8,128)S(1)}, f32[944,128]{1,0:T(8,128)S(1)}, u32[]{:S(2)}, u32[]{:S(2)}) collective-permute-start(f32[944,128]{1,0:T(8,128)S(1)} %get-tuple-element.21), channel_id=1, source_target_pairs={{0,4},{4,8},{8,12},{12,16},{16,20},{20,24},{24,28},{1,5},{5,9},{9,... | collective-permute-start | bytes 1449992 | tf_op jit(solution)/shard_map/ppermute | solution.py:655
  23.3 1.3 %collective-permute-start.5 = (f32[944,128]{1,0:T(8,128)S(1)}, f32[944,128]{1,0:T(8,128)S(1)}, u32[]{:S(2)}, u32[]{:S(2)}) collective-permute-start(f32[944,128]{1,0:T(8,128)S(1)} %get-tuple-element.22), channel_id=1, source_target_pairs={{4,0},{8,4},{12,8},{16,12},{20,16},{24,20},{28,24},{5,1},{9,5},{13... | collective-permute-start | bytes 1449992 | tf_op jit(solution)/shard_map/ppermute | solution.py:655
  24.6 0.1 collective-permute-done.4.low_ref
  24.7 4.1 %collective-permute-done.5.high_ref = f32[944,128]{1,0:T(8,128)S(1)} collective-permute-done((f32[944,128]{1,0:T(8,128)S(1)}, f32[944,128]{1,0:T(8,128)S(1)}, u32[]{:S(2)}, u32[]{:S(2)}) %collective-permute-start.5) | collective-permute-done | bytes 483360 | tf_op jit(solution)/shard_map/ppermute | solution.py:655
  28.8 12.3 %shard_map.30 = (f32[16,16,128]{2,1,0:T(8,128)S(1)}, f32[8,8,128]{2,1,0:T(8,128)S(1)}, f32[16,128]{1,0:T(8,128)S(1)}) custom-call(f32[944,128]{1,0:T(8,128)S(1)} %collective-permute-done.4.low_ref, f32[944,128]{1,0:T(8,128)S(1)} %collective-permute-done.5.high_ref, f32[82,16,128]{2,1,0:T(8,128)S(1)} %get-tuple-element.23.main_ref, ...), custom_call_target="tpu_custom_call" | custom-call | tf_op jit(solution)/shard_map/pallas_call | solution.py:642
  41.1 2.1 %collective-permute-start.7 = (f32[16,128]{1,0:T(8,128)S(1)}, f32[16,128]{1,0:T(8,128)S(1)}, u32[]{:S(2)}, u32[]{:S(2)}) collective-permute-start(f32[16,128]{1,0:T(8,128)S(1)} %get-tuple-element.24.own_ref), channel_id=1, source_target_pairs={{32,0},{64,32},{96,64},{128,96},{160,128},{192,160},{224,192},{256... | collective-permute-start | bytes 24584 | tf_op jit(solution)/shard_map/ppermute | solution.py:655
  43.2 4.9 %collective-permute-start.6 = (f32[16,128]{1,0:T(8,128)S(1)}, f32[16,128]{1,0:T(8,128)S(1)}, u32[]{:S(2)}, u32[]{:S(2)}) collective-permute-start(f32[16,128]{1,0:T(8,128)S(1)} %get-tuple-element.24.own_ref), channel_id=1, source_target_pairs={{0,32},{32,64},{64,96},{96,128},{128,160},{160,192},{192,224},{224... | collective-permute-start | bytes 24584 | tf_op jit(solution)/shard_map/ppermute | solution.py:655
  48.1 0.0 collective-permute-done.7.high_ref
  48.1 1.3 %collective-permute-done.6.low_ref = f32[16,128]{1,0:T(8,128)S(1)} collective-permute-done((f32[16,128]{1,0:T(8,128)S(1)}, f32[16,128]{1,0:T(8,128)S(1)}, u32[]{:S(2)}, u32[]{:S(2)}) %collective-permute-start.6) | collective-permute-done | bytes 8224 | tf_op jit(solution)/shard_map/ppermute | solution.py:655
  49.5 24.9 %all_to_all.10 = f32[32,32,128]{2,1,0:T(8,128)S(1)} all-to-all(f32[32,32,128]{2,1,0:T(8,128)S(1)} %shard_map.31), channel_id=1, replica_groups=mesh['gx'=16,'gy'=8,'gz'=4] {'gy','gz'}, dimensions={0} | all-to-all | bytes 1048576 | tf_op jit(solution)/shard_map/all_to_all | solution.py:687
  74.4 2.2 %shard_map.32 = (f32[4,32,128]{2,1,0:T(8,128)S(1)}, f32[16,32,128]{2,1,0:T(8,128)S(1)}) custom-call(f32[1024,128]{1,0:T(8,128)S(1)} %bitcast.1), custom_call_target="tpu_custom_call" | custom-call | tf_op jit(solution)/shard_map/pallas_call | solution.py:642
  76.6 35.7 %all_to_all.11.gathered_ref = f32[16,32,128]{2,1,0:T(8,128)S(1)} all-to-all(f32[16,32,128]{2,1,0:T(8,128)S(1)} %get-tuple-element.25), channel_id=1, replica_groups=mesh['gx'=16,'gy'=8,'gz'=4] {'gx'}, dimensions={0} | all-to-all | bytes 524288 | tf_op jit(solution)/shard_map/all_to_all | solution.py:696
  112.4 4.5 %shard_map.33 = f32[16,16,128]{2,1,0:T(8,128)} custom-call(f32[16,32,128]{2,1,0:T(8,128)S(1)} %all_to_all.11.gathered_ref, f32[16,16,128]{2,1,0:T(8,128)S(1)} %get-tuple-element.26.u0_ref, f32[8,8,128]{2,1,0:T(8,128)S(1)} %get-tuple-element.27.u1_ref, f32[4,32,128]{2,1,0:T(8,128)S(1)} %get-tuple-element.28.u2_ref), custom_call_target="tpu_custom_call" | custom-call | tf_op jit(solution)/shard_map/pallas_call | solution.py:642
  (4 shorter events, 0.1 us)
Async XLA Ops:
  0.0 1.0 copy-start
  1.1 10.5 %collective-permute-start = (f32[25,16,128]{2,1,0:T(8,128)S(1)}, f32[25,16,128]{2,1,0:T(8,128)S(1)}, u32[]{:S(2)}, u32[]{:S(2)}) collective-permute-start(f32[25,16,128]{2,1,0:T(8,128)S(1)} %pad_maximum_fusion), channel_id=1, source_target_pairs={{0,32},{32,64},{64,96},{96,128},{128,160},{160,192},{192,224},{224... | collective-permute-start | bytes 614408 | tf_op jit(solution)/shard_map/ppermute | solution.py:655
  4.9 8.8 %copy-start.1 = (f32[16,16,128]{2,1,0:T(8,128)S(1)}, f32[16,16,128]{2,1,0:T(8,128)}, u32[]{:S(2)}) copy-start(f32[16,16,128]{2,1,0:T(8,128)} %f_ref.1) | copy-start | bytes 393220
  4.9 8.7 %collective-permute-start.1 = (f32[25,16,128]{2,1,0:T(8,128)S(1)}, f32[25,16,128]{2,1,0:T(8,128)S(1)}, u32[]{:S(2)}, u32[]{:S(2)}) collective-permute-start(f32[25,16,128]{2,1,0:T(8,128)S(1)} %pad_maximum_fusion.1), channel_id=1, source_target_pairs={{32,0},{64,32},{96,64},{128,96},{160,128},{192,160},{224,192},{256... | collective-permute-start | bytes 614408 | tf_op jit(solution)/shard_map/ppermute | solution.py:655
  13.9 6.4 %collective-permute-start.2 = (f32[11,16,128]{2,1,0:T(8,128)S(1)}, f32[11,16,128]{2,1,0:T(8,128)S(1)}, u32[]{:S(2)}, u32[]{:S(2)}) collective-permute-start(f32[11,16,128]{2,1,0:T(8,128)S(1)} %get-tuple-element.19), channel_id=1, source_target_pairs={{1,0},{2,1},{3,2},{5,4},{6,5},{7,6},{9,8},{10,9},{11,10},{13,12},{... | collective-permute-start | bytes 270344 | tf_op jit(solution)/shard_map/ppermute | solution.py:655
  15.2 6.7 %collective-permute-start.3 = (f32[11,16,128]{2,1,0:T(8,128)S(1)}, f32[11,16,128]{2,1,0:T(8,128)S(1)}, u32[]{:S(2)}, u32[]{:S(2)}) collective-permute-start(f32[11,16,128]{2,1,0:T(8,128)S(1)} %get-tuple-element.20), channel_id=1, source_target_pairs={{0,1},{1,2},{2,3},{4,5},{5,6},{6,7},{8,9},{9,10},{10,11},{12,13},{... | collective-permute-start | bytes 270344 | tf_op jit(solution)/shard_map/ppermute | solution.py:655
  22.0 2.8 %collective-permute-start.4 = (f32[944,128]{1,0:T(8,128)S(1)}, f32[944,128]{1,0:T(8,128)S(1)}, u32[]{:S(2)}, u32[]{:S(2)}) collective-permute-start(f32[944,128]{1,0:T(8,128)S(1)} %get-tuple-element.21), channel_id=1, source_target_pairs={{0,4},{4,8},{8,12},{12,16},{16,20},{20,24},{24,28},{1,5},{5,9},{9,... | collective-permute-start | bytes 1449992 | tf_op jit(solution)/shard_map/ppermute | solution.py:655
  23.3 5.5 %collective-permute-start.5 = (f32[944,128]{1,0:T(8,128)S(1)}, f32[944,128]{1,0:T(8,128)S(1)}, u32[]{:S(2)}, u32[]{:S(2)}) collective-permute-start(f32[944,128]{1,0:T(8,128)S(1)} %get-tuple-element.22), channel_id=1, source_target_pairs={{4,0},{8,4},{12,8},{16,12},{20,16},{24,20},{28,24},{5,1},{9,5},{13... | collective-permute-start | bytes 1449992 | tf_op jit(solution)/shard_map/ppermute | solution.py:655
  41.1 7.0 %collective-permute-start.7 = (f32[16,128]{1,0:T(8,128)S(1)}, f32[16,128]{1,0:T(8,128)S(1)}, u32[]{:S(2)}, u32[]{:S(2)}) collective-permute-start(f32[16,128]{1,0:T(8,128)S(1)} %get-tuple-element.24.own_ref), channel_id=1, source_target_pairs={{32,0},{64,32},{96,64},{128,96},{160,128},{192,160},{224,192},{256... | collective-permute-start | bytes 24584 | tf_op jit(solution)/shard_map/ppermute | solution.py:655
  43.2 6.2 %collective-permute-start.6 = (f32[16,128]{1,0:T(8,128)S(1)}, f32[16,128]{1,0:T(8,128)S(1)}, u32[]{:S(2)}, u32[]{:S(2)}) collective-permute-start(f32[16,128]{1,0:T(8,128)S(1)} %get-tuple-element.24.own_ref), channel_id=1, source_target_pairs={{0,32},{32,64},{64,96},{96,128},{128,160},{160,192},{192,224},{224... | collective-permute-start | bytes 24584 | tf_op jit(solution)/shard_map/ppermute | solution.py:655

commit v2 on v1

--- a/solution.py
+++ b/solution.py
@@ -209,6 +209,7 @@
     f_ref, b_ref, low_ref, high_ref, main_ref, left_ref, right_ref, down_ref, up_ref
 ):
     lane = iota((BLOCK, 128), 1)
+    even = lax.rem(lax.axis_index("gz"), 2) == 0
 
     def source(index):
         if index < F_HALO:
@@ -240,11 +241,18 @@
             turned = pltpu.roll(plane, 16 * slot, 1) if slot else plane
             left = jnp.where((lane >> 4) == slot, turned, left)
             right = jnp.where((lane >> 4) == ((slot - 1) & 7), turned, right)
-        left_ref[group] = left
-        right_ref[group] = right
-
-
-def join_kernel(down_ref, up_ref, after_ref, before_ref, down_out, up_out):
+        left_ref[group] = jnp.where(even, right, left)
+        right_ref[group] = jnp.where(even, left, right)
+
+
+def join_kernel(
+    down_ref, up_ref, first_ref, second_ref, down_out, up_out, after_ref, before_ref
+):
+    even = lax.rem(lax.axis_index("gz"), 2) == 0
+    for group in range(GROUPS):
+        first, second = first_ref[group], second_ref[group]
+        after_ref[group] = jnp.where(even, first, second)
+        before_ref[group] = jnp.where(even, second, first)
     down_out[0:PACKED] = down_ref[...]
     up_out[0:PACKED] = up_ref[...]
     for side, strips in enumerate((after_ref, before_ref)):
@@ -270,7 +278,12 @@
         even = ((iota(after.shape, 1) >> 4) & 1) == 0
         return jnp.where(even, after, before), jnp.where(even, before, after)
 
+    at_y = lax.axis_index("gy")
+    low_there = jnp.where(at_y > 0, 1.0, 0.0)
+    high_there = jnp.where(at_y < lax.axis_size("gy") - 1, 1.0, 0.0)
+
     def place(target, plane, index, scale):
+        low_scale, high_scale = low_there * scale, high_there * scale
         group, slot = index // 8, index % 8
         count, start = COUNTS[index], OFFSETS[index]
         main, side = target
@@ -279,17 +292,17 @@
         main[plane, last : last + BLOCK] = blank
         main[plane, own:last] = main_ref[index] * scale
         if count:
-            main[plane, own - count : own] = low_ref[start : start + count] * scale
-            main[plane, last : last + count] = high_ref[start : start + count] * scale
-
-        def turned(pair):
+            main[plane, own - count : own] = low_ref[start : start + count] * low_scale
+            main[plane, last : last + count] = high_ref[start : start + count] * high_scale
+
+        def turned(pair, scale):
             value = pair[slot & 1]
             if slot:
                 value = pltpu.roll(value, 128 - 16 * slot, 1)
             lane = iota(value.shape, 1)
             return jnp.where((lane < 16) | (lane >= 112), value, 0.0) * scale
 
-        side[plane, own:last] = turned(unpack(after_ref[group], before_ref[group]))
+        side[plane, own:last] = turned(unpack(after_ref[group], before_ref[group]), scale)
         rows = STRIP_ROWS[group]
         if rows < BLOCK:
             side[plane, first:own] = blank
@@ -297,9 +310,11 @@
         if rows:
             start = STRIP_OFFSETS[group]
             beyond = slice(start, start + rows), slice(start + SIDE, start + SIDE + rows)
-            side[plane, own - rows : own] = turned(unpack(low_ref[beyond[0]], low_ref[beyond[1]]))
+            side[plane, own - rows : own] = turned(
+                unpack(low_ref[beyond[0]], low_ref[beyond[1]]), low_scale
+            )
             side[plane, last : last + rows] = turned(
-                unpack(high_ref[beyond[0]], high_ref[beyond[1]])
+                unpack(high_ref[beyond[0]], high_ref[beyond[1]]), high_scale
             )
 
     for index in range(F_PLANES):
@@ -655,6 +670,18 @@
     return lax.ppermute(value, axis, pairs)
 
 
+def around(value, axis, step):
+    count = lax.axis_size(axis)
+    return lax.ppermute(value, axis, [(i, (i + step) % count) for i in range(count)])
+
+
+def swap(value, axis, first):
+    count = lax.axis_size(axis)
+    lower = range(first, count - 1, 2)
+    pairs = [(i, i + 1) for i in lower] + [(i + 1, i) for i in lower]
+    return lax.ppermute(value, axis, pairs)
+
+
 def on_device(right_side, conductivity):
     f, b = right_side, conductivity
     upper = jnp.concatenate([f[BLOCK - F_HALO :], b[BLOCK - B_HALO :]], axis=0)
@@ -666,9 +693,11 @@
     main, left, right, down, up = call(
         pack_kernel, 4, [(PLANES, BLOCK, 128), strip, strip, packed, packed], [], f, b, low, high
     )
-    after, before = shift(left, "gz", -1), shift(right, "gz", 1)
-    down, up = call(join_kernel, 4, [(PAYLOAD, 128)] * 2, [], down, up, after, before)
-    low, high = shift(up, "gy", 1), shift(down, "gy", -1)
+    first, second = swap(left, "gz", 0), swap(right, "gz", 1)
+    down, up, after, before = call(
+        join_kernel, 4, [(PAYLOAD, 128)] * 2 + [strip] * 2, [], down, up, first, second
+    )
+    low, high = around(up, "gy", 1), around(down, "gy", -1)
 
     u0, u1, coarse = call(
         fine_kernel,

time: 117 us -> 114 us (0.974)
  blocking collectives: 60.7 us -> 55.6 us
  waiting for transfers between devices: 11.4 us -> 15 us
  starting transfers between devices: 24.2 us -> 22.8 us
    ppermute x0 -> x4, waiting for transfers between devices: none -> 8.77 us  [the longest x2 6.42 us: around(): lax.ppermute(value, axis, [(i, (i + step) % count) for i in range(count)])]
    ppermute x8 -> x4, starting transfers between devices: 24.2 us -> 15.8 us  [shift(): return lax.ppermute(value, axis, pairs)]
    ppermute x0 -> x4, starting transfers between devices: none -> 7.03 us  [the longest x2 4.07 us: swap(): return lax.ppermute(value, axis, pairs)]
    all_to_all x1, blocking collectives: 24.9 us -> 19.7 us  [on_device(): slab = lax.all_to_all(slab, ('gy', 'gz'), 0, 0, tiled=True)]
    ppermute x8 -> x4, waiting for transfers between devices: 11.4 us -> 6.21 us  [shift(): return lax.ppermute(value, axis, pairs)]
  transfers between devices with their start and end apart: 8 -> 8, of which waited for: 7 -> 5; matrix products, arithmetic and copies ran while one was open for 0% -> 0% of each run, Pallas kernels for 0% -> 0%
where the time goes in v2:
time: 114 us
  blocking collectives  55.6 us (49%)
  starting transfers between devices  22.8 us (20%)
  Pallas kernels  19.4 us (17%)
  waiting for transfers between devices  15 us (13%)
    all_to_all x1, blocking collectives, on_device(): whole = lax.all_to_all(coarse, 'gx', 0, 0, tiled=True)  35.9 us
    all_to_all x1, blocking collectives, on_device(): slab = lax.all_to_all(slab, ('gy', 'gz'), 0, 0, tiled=True)  19.7 us
    pallas_call x6, Pallas kernels, call(): pl.pallas_call(kernel, out_shape=[jax.ShapeDtypeStruct(shape, F32) for sh...  19.4 us
    ppermute x4, starting transfers between devices, shift(): return lax.ppermute(value, axis, pairs)  15.8 us
    ppermute x2, waiting for transfers between devices, around(): lax.ppermute(value, axis, [(i, (i + step) % count) for i in range(count)])  6.42 us
    ppermute x4, waiting for transfers between devices, shift(): return lax.ppermute(value, axis, pairs)  6.21 us
    ppermute x2, starting transfers between devices, swap(): return lax.ppermute(value, axis, pairs)  4.07 us
    ppermute x2, starting transfers between devices, around(): lax.ppermute(value, axis, [(i, (i + step) % count) for i in range(count)])  2.96 us
  transfers between devices with their start and end apart: 8, of which 5 were waited for; matrix products, arithmetic and copies ran while one was open for 0% of the time, Pallas kernels for 0%

profile of v2, /device:TPU:32, one launch (start us, length us, event | category | flops | bytes accessed | tf_op | source)
XLA Modules:
  0.0 113.9 jit_solution(4973209157558783119)
XLA Ops:
  0.0 0.0 copy-start
  0.0 1.0 fusion
  1.0 0.0 copy-done
  1.1 3.8 %collective-permute-start = (f32[25,16,128]{2,1,0:T(8,128)S(1)}, f32[25,16,128]{2,1,0:T(8,128)S(1)}, u32[]{:S(2)}, u32[]{:S(2)}) collective-permute-start(f32[25,16,128]{2,1,0:T(8,128)S(1)} %pad_maximum_fusion), channel_id=1, source_target_pairs={{0,32},{32,64},{64,96},{96,128},{128,160},{160,192},{192,224},{224... | collective-permute-start | bytes 614408 | tf_op jit(solution)/shard_map/ppermute | solution.py:670
  4.9 0.0 copy-start.1
  4.9 5.0 %collective-permute-start.1 = (f32[25,16,128]{2,1,0:T(8,128)S(1)}, f32[25,16,128]{2,1,0:T(8,128)S(1)}, u32[]{:S(2)}, u32[]{:S(2)}) collective-permute-start(f32[25,16,128]{2,1,0:T(8,128)S(1)} %pad_maximum_fusion.1), channel_id=1, source_target_pairs={{32,0},{64,32},{96,64},{128,96},{160,128},{192,160},{224,192},{256... | collective-permute-start | bytes 614408 | tf_op jit(solution)/shard_map/ppermute | solution.py:670
  9.9 1.6 %collective-permute-done.low_ref = f32[25,16,128]{2,1,0:T(8,128)S(1)} collective-permute-done((f32[25,16,128]{2,1,0:T(8,128)S(1)}, f32[25,16,128]{2,1,0:T(8,128)S(1)}, u32[]{:S(2)}, u32[]{:S(2)}) %collective-permute-start) | collective-permute-done | bytes 204832 | tf_op jit(solution)/shard_map/ppermute | solution.py:670
  11.5 2.1 %collective-permute-done.1.high_ref = f32[25,16,128]{2,1,0:T(8,128)S(1)} collective-permute-done((f32[25,16,128]{2,1,0:T(8,128)S(1)}, f32[25,16,128]{2,1,0:T(8,128)S(1)}, u32[]{:S(2)}, u32[]{:S(2)}) %collective-permute-start.1) | collective-permute-done | bytes 204832 | tf_op jit(solution)/shard_map/ppermute | solution.py:670
  13.7 0.0 copy-done.1
  13.7 0.2 shard_map.28
  13.9 3.4 %collective-permute-start.2 = (f32[11,16,128]{2,1,0:T(8,128)S(1)}, f32[11,16,128]{2,1,0:T(8,128)S(1)}, u32[]{:S(2)}, u32[]{:S(2)}) collective-permute-start(f32[11,16,128]{2,1,0:T(8,128)S(1)} %get-tuple-element.21), channel_id=1, source_target_pairs={{0,1},{2,3},{1,0},{3,2},{4,5},{6,7},{5,4},{7,6},{8,9},{10,11},{9,8... | collective-permute-start | bytes 270344 | tf_op jit(solution)/shard_map/ppermute | solution.py:682
  17.3 0.7 collective-permute-start.3
  18.0 2.3 %collective-permute-done.2.first_ref = f32[11,16,128]{2,1,0:T(8,128)S(1)} collective-permute-done((f32[11,16,128]{2,1,0:T(8,128)S(1)}, f32[11,16,128]{2,1,0:T(8,128)S(1)}, u32[]{:S(2)}, u32[]{:S(2)}) %collective-permute-start.2) | collective-permute-done | bytes 90144 | tf_op jit(solution)/shard_map/ppermute | solution.py:682
  20.3 0.0 collective-permute-done.3.second_ref
  20.3 0.1 shard_map.29
  20.4 0.0 collective-permute-start.4
  20.5 2.9 %collective-permute-start.5 = (f32[944,128]{1,0:T(8,128)S(1)}, f32[944,128]{1,0:T(8,128)S(1)}, u32[]{:S(2)}, u32[]{:S(2)}) collective-permute-start(f32[944,128]{1,0:T(8,128)S(1)} %get-tuple-element.24), channel_id=1, source_target_pairs={{0,28},{4,0},{8,4},{12,8},{16,12},{20,16},{24,20},{28,24},{1,29},{... | collective-permute-start | bytes 1449992 | tf_op jit(solution)/shard_map/ppermute | solution.py:675
  23.4 6.4 %collective-permute-done.4.low_ref = f32[944,128]{1,0:T(8,128)S(1)} collective-permute-done((f32[944,128]{1,0:T(8,128)S(1)}, f32[944,128]{1,0:T(8,128)S(1)}, u32[]{:S(2)}, u32[]{:S(2)}) %collective-permute-start.4) | collective-permute-done | bytes 483360 | tf_op jit(solution)/shard_map/ppermute | solution.py:675
  29.8 0.0 collective-permute-done.5.high_ref
  29.8 12.3 %shard_map.30 = (f32[16,16,128]{2,1,0:T(8,128)S(1)}, f32[8,8,128]{2,1,0:T(8,128)S(1)}, f32[16,128]{1,0:T(8,128)S(1)}) custom-call(f32[944,128]{1,0:T(8,128)S(1)} %collective-permute-done.4.low_ref, f32[944,128]{1,0:T(8,128)S(1)} %collective-permute-done.5.high_ref, f32[82,16,128]{2,1,0:T(8,128)S(1)} %get-tuple-element.25.main_ref, ...), custom_call_target="tpu_custom_call" | custom-call | tf_op jit(solution)/shard_map/pallas_call | solution.py:657
  42.1 3.9 %collective-permute-start.7 = (f32[16,128]{1,0:T(8,128)S(1)}, f32[16,128]{1,0:T(8,128)S(1)}, u32[]{:S(2)}, u32[]{:S(2)}) collective-permute-start(f32[16,128]{1,0:T(8,128)S(1)} %get-tuple-element.28.own_ref), channel_id=1, source_target_pairs={{32,0},{64,32},{96,64},{128,96},{160,128},{192,160},{224,192},{256... | collective-permute-start | bytes 24584 | tf_op jit(solution)/shard_map/ppermute | solution.py:670
  46.0 3.1 %collective-permute-start.6 = (f32[16,128]{1,0:T(8,128)S(1)}, f32[16,128]{1,0:T(8,128)S(1)}, u32[]{:S(2)}, u32[]{:S(2)}) collective-permute-start(f32[16,128]{1,0:T(8,128)S(1)} %get-tuple-element.28.own_ref), channel_id=1, source_target_pairs={{0,32},{32,64},{64,96},{96,128},{128,160},{160,192},{192,224},{224... | collective-permute-start | bytes 24584 | tf_op jit(solution)/shard_map/ppermute | solution.py:670
  49.1 0.0 collective-permute-done.7.high_ref
  49.1 2.4 %collective-permute-done.6.low_ref = f32[16,128]{1,0:T(8,128)S(1)} collective-permute-done((f32[16,128]{1,0:T(8,128)S(1)}, f32[16,128]{1,0:T(8,128)S(1)}, u32[]{:S(2)}, u32[]{:S(2)}) %collective-permute-start.6) | collective-permute-done | bytes 8224 | tf_op jit(solution)/shard_map/ppermute | solution.py:670
  51.6 19.7 %all_to_all.10 = f32[32,32,128]{2,1,0:T(8,128)S(1)} all-to-all(f32[32,32,128]{2,1,0:T(8,128)S(1)} %shard_map.31), channel_id=1, replica_groups=mesh['gx'=16,'gy'=8,'gz'=4] {'gy','gz'}, dimensions={0} | all-to-all | bytes 1048576 | tf_op jit(solution)/shard_map/all_to_all | solution.py:716
  71.3 2.2 %shard_map.32 = (f32[4,32,128]{2,1,0:T(8,128)S(1)}, f32[16,32,128]{2,1,0:T(8,128)S(1)}) custom-call(f32[1024,128]{1,0:T(8,128)S(1)} %bitcast.1), custom_call_target="tpu_custom_call" | custom-call | tf_op jit(solution)/shard_map/pallas_call | solution.py:657
  73.5 35.9 %all_to_all.11.gathered_ref = f32[16,32,128]{2,1,0:T(8,128)S(1)} all-to-all(f32[16,32,128]{2,1,0:T(8,128)S(1)} %get-tuple-element.29), channel_id=1, replica_groups=mesh['gx'=16,'gy'=8,'gz'=4] {'gx'}, dimensions={0} | all-to-all | bytes 524288 | tf_op jit(solution)/shard_map/all_to_all | solution.py:725
  109.4 4.5 %shard_map.33 = f32[16,16,128]{2,1,0:T(8,128)} custom-call(f32[16,32,128]{2,1,0:T(8,128)S(1)} %all_to_all.11.gathered_ref, f32[16,16,128]{2,1,0:T(8,128)S(1)} %get-tuple-element.30.u0_ref, f32[8,8,128]{2,1,0:T(8,128)S(1)} %get-tuple-element.31.u1_ref, f32[4,32,128]{2,1,0:T(8,128)S(1)} %get-tuple-element.32.u2_ref), custom_call_target="tpu_custom_call" | custom-call | tf_op jit(solution)/shard_map/pallas_call | solution.py:657
  (4 shorter events, 0.1 us)
Async XLA Ops:
  0.0 1.0 copy-start
  1.1 10.5 %collective-permute-start = (f32[25,16,128]{2,1,0:T(8,128)S(1)}, f32[25,16,128]{2,1,0:T(8,128)S(1)}, u32[]{:S(2)}, u32[]{:S(2)}) collective-permute-start(f32[25,16,128]{2,1,0:T(8,128)S(1)} %pad_maximum_fusion), channel_id=1, source_target_pairs={{0,32},{32,64},{64,96},{96,128},{128,160},{160,192},{192,224},{224... | collective-permute-start | bytes 614408 | tf_op jit(solution)/shard_map/ppermute | solution.py:670
  4.9 8.8 %copy-start.1 = (f32[16,16,128]{2,1,0:T(8,128)S(1)}, f32[16,16,128]{2,1,0:T(8,128)}, u32[]{:S(2)}) copy-start(f32[16,16,128]{2,1,0:T(8,128)} %f_ref.1) | copy-start | bytes 393220
  4.9 8.7 %collective-permute-start.1 = (f32[25,16,128]{2,1,0:T(8,128)S(1)}, f32[25,16,128]{2,1,0:T(8,128)S(1)}, u32[]{:S(2)}, u32[]{:S(2)}) collective-permute-start(f32[25,16,128]{2,1,0:T(8,128)S(1)} %pad_maximum_fusion.1), channel_id=1, source_target_pairs={{32,0},{64,32},{96,64},{128,96},{160,128},{192,160},{224,192},{256... | collective-permute-start | bytes 614408 | tf_op jit(solution)/shard_map/ppermute | solution.py:670
  13.9 6.4 %collective-permute-start.2 = (f32[11,16,128]{2,1,0:T(8,128)S(1)}, f32[11,16,128]{2,1,0:T(8,128)S(1)}, u32[]{:S(2)}, u32[]{:S(2)}) collective-permute-start(f32[11,16,128]{2,1,0:T(8,128)S(1)} %get-tuple-element.21), channel_id=1, source_target_pairs={{0,1},{2,3},{1,0},{3,2},{4,5},{6,7},{5,4},{7,6},{8,9},{10,11},{9,8... | collective-permute-start | bytes 270344 | tf_op jit(solution)/shard_map/ppermute | solution.py:682
  17.3 3.0 %collective-permute-start.3 = (f32[11,16,128]{2,1,0:T(8,128)S(1)}, f32[11,16,128]{2,1,0:T(8,128)S(1)}, u32[]{:S(2)}, u32[]{:S(2)}) collective-permute-start(f32[11,16,128]{2,1,0:T(8,128)S(1)} %get-tuple-element.22), channel_id=1, source_target_pairs={{1,2},{2,1},{5,6},{6,5},{9,10},{10,9},{13,14},{14,13},{17,18},{18,... | collective-permute-start | bytes 270344 | tf_op jit(solution)/shard_map/ppermute | solution.py:682
  20.4 9.4 %collective-permute-start.4 = (f32[944,128]{1,0:T(8,128)S(1)}, f32[944,128]{1,0:T(8,128)S(1)}, u32[]{:S(2)}, u32[]{:S(2)}) collective-permute-start(f32[944,128]{1,0:T(8,128)S(1)} %get-tuple-element.23), channel_id=1, source_target_pairs={{0,4},{4,8},{8,12},{12,16},{16,20},{20,24},{24,28},{28,0},{1,5},{5... | collective-permute-start | bytes 1449992 | tf_op jit(solution)/shard_map/ppermute | solution.py:675
  20.5 9.4 %collective-permute-start.5 = (f32[944,128]{1,0:T(8,128)S(1)}, f32[944,128]{1,0:T(8,128)S(1)}, u32[]{:S(2)}, u32[]{:S(2)}) collective-permute-start(f32[944,128]{1,0:T(8,128)S(1)} %get-tuple-element.24), channel_id=1, source_target_pairs={{0,28},{4,0},{8,4},{12,8},{16,12},{20,16},{24,20},{28,24},{1,29},{... | collective-permute-start | bytes 1449992 | tf_op jit(solution)/shard_map/ppermute | solution.py:675
  42.1 7.0 %collective-permute-start.7 = (f32[16,128]{1,0:T(8,128)S(1)}, f32[16,128]{1,0:T(8,128)S(1)}, u32[]{:S(2)}, u32[]{:S(2)}) collective-permute-start(f32[16,128]{1,0:T(8,128)S(1)} %get-tuple-element.28.own_ref), channel_id=1, source_target_pairs={{32,0},{64,32},{96,64},{128,96},{160,128},{192,160},{224,192},{256... | collective-permute-start | bytes 24584 | tf_op jit(solution)/shard_map/ppermute | solution.py:670
  46.0 5.5 %collective-permute-start.6 = (f32[16,128]{1,0:T(8,128)S(1)}, f32[16,128]{1,0:T(8,128)S(1)}, u32[]{:S(2)}, u32[]{:S(2)}) collective-permute-start(f32[16,128]{1,0:T(8,128)S(1)} %get-tuple-element.28.own_ref), channel_id=1, source_target_pairs={{0,32},{32,64},{64,96},{96,128},{128,160},{160,192},{192,224},{224... | collective-permute-start | bytes 24584 | tf_op jit(solution)/shard_map/ppermute | solution.py:670

commit v3 on v2

--- a/solution.py
+++ b/solution.py
@@ -81,6 +81,12 @@
     def scratch(columns, planes, rows):
         return [(planes, rows + 16, 128)] * (len(Level.names) * columns)
 
+    def low(self, row):
+        return row - 1
+
+    def high(self, row):
+        return row + 1
+
     def at(self, refs, plane, row):
         return [ref[plane, row : row + 8] for ref in refs]
 
@@ -114,15 +120,15 @@
                     ref[plane] = jnp.zeros((rows + 16, 128), F32)
 
     def before(self, plane, rows):
-        for row in range(8, rows + 8, 8):
+        for row in rows:
             near = zip(self.at(self.b, plane, row), self.at(self.b, plane + 1, row))
             self.put(self.fx, plane, row, [own + other for own, other in near])
 
     def setup(self, plane, rows, red):
-        for row in range(8, rows + 8, 8):
+        for row in rows:
             b = self.at(self.b, plane, row)
             x_low, x_high = self.at(self.b, plane - 1, row), self.at(self.b, plane + 1, row)
-            y_low, y_high = self.at(self.b, plane, row - 1), self.at(self.b, plane, row + 1)
+            y_low, y_high = self.at(self.b, plane, self.low(row)), self.at(self.b, plane, self.high(row))
             z_low, z_high = self.turn(b, -1), self.turn(b, 1)
             g = self.at(self.g, plane, row)
             for column in range(self.columns):
@@ -166,7 +172,8 @@
         for column in range(self.columns):
             ref, fx, fy = source[column], self.fx[column], self.fy[column]
             along_x = load(fx, step) * load(ref, step + 1) + load(fx, step - 1) * load(ref, step - 1)
-            low, high = slice(row - 1, row + 7), slice(row + 1, row + 9)
+            low = slice(self.low(row), self.low(row) + 8)
+            high = slice(self.high(row), self.high(row) + 8)
             plane = base + step
             along_y = load(fy, step) * ref[plane, high] + fy[plane, low] * ref[plane, low]
             along_z = face_z[column] * z_high[column] + z_low[column]
@@ -323,14 +330,14 @@
         place(fine.b, index - F_PLANES, index, 1.0)
 
     fine.clear(B_PLANES, ROWS, (0, B_PLANES - 1))
-    fine.before(0, ROWS)
+    every = range(8, ROWS + 8, 8)
+    fine.before(0, every)
 
     @pl.loop(1, B_PLANES - 1, step=4)
     def _(plane):
         for index in range(4):
-            fine.setup(plane + index, ROWS, index & 1)
-
-    every = range(8, ROWS + 8, 8)
+            fine.setup(plane + index, every, index & 1)
+
     inner = range(16, ROWS, 8)
     for step in range(3):
         beside = 2 - step
@@ -384,12 +391,12 @@
         middle.g[0][plane, 12:28] = g_next[16 * (plane - 2) : 16 * (plane - 1)]
     for plane in range(1, 19):
         middle.b[0][plane, 8:32] = b_next[24 * (plane - 1) : 24 * plane]
-    middle.before(1, 24)
+    middle.before(1, range(8, 32, 8))
 
     @pl.loop(2, 18, step=4)
     def _(plane):
         for index in range(4):
-            middle.setup(plane + index, 24, index & 1)
+            middle.setup(plane + index, range(8, 32, 8), index & 1)
 
     for step in range(3):
 
@@ -400,96 +407,145 @@
     for plane in range(8):
         u1_ref[plane] = middle.k[0][plane + 6, 16:24]
     for index in range(4):
+        at = 32 * index
         (first,) = middle.rest(2 * index + 6, 16)
         (second,) = middle.rest(2 * index + 7, 16)
-        collect[8 * index : 8 * index + 8] = 0.5 * (first + second)
-    for index in range(6):
-        first, second = middle.b[0][2 * index + 4, 16:24], middle.b[0][2 * index + 5, 16:24]
-        collect[8 * index + 32 : 8 * index + 40] = 0.125 * (first + second)
-    collect[80:128] = jnp.zeros((48, 128), F32)
+        collect[at : at + 8] = 0.5 * (first + second)
+        first, second = middle.b[0][2 * index + 6, 14:26], middle.b[0][2 * index + 7, 14:26]
+        collect[at + 8 : at + 20] = 0.125 * (first + second)
+        collect[at + 20 : at + 32] = jnp.zeros((12, 128), F32)
     out = jnp.zeros((16, 128), F32)
-    for part in range(4):
-        rows = collect[pl.ds(2 * part, 16, stride=8), :]
-        rows = rows + collect[pl.ds(2 * part + 1, 16, stride=8), :]
-        out = out + split_matmul(rows, pair_selector(128, 0, 128, 32 * part, 32))
-    coarse_ref[...] = out
-
-
-def spread_kernel(low_ref, own_ref, high_ref, out_ref, rows):
-    rows[0:4] = low_ref[0:4]
-    rows[4:8] = own_ref[0:4]
-    rows[8:12] = high_ref[0:4]
-    rows[12:17] = low_ref[4:9]
-    rows[17:21] = own_ref[5:9]
-    rows[21:26] = high_ref[5:10]
-    rows[26:32] = jnp.zeros((6, 128), F32)
-    value = rows[...]
-    for index in range(32):
-        out_ref[index] = value
-
-
-def slab_kernel(gathered_ref, u2_ref, coarse_ref, *scratch):
-    slab = Level(scratch[: len(Level.names)], 1, True)
-    rest, sums = scratch[len(Level.names) :]
-    row = iota((4, 8, 128), 1)
-    lane = iota((4, 8, 128), 2)
-    group = lane >> 5
-    turn = (group - row) & 3
-
-    def exchange(value):
-        value = value.reshape(4, 8, 128)
-        out = value
-        for d in (1, 2, 3):
-            moved = pltpu.roll(value, 32 * d, 2)
-            near = pltpu.roll(moved, 8 - d, 1)
-            far = pltpu.roll(moved, 4 - d, 1)
-            out = jnp.where(turn == d, jnp.where(group >= d, near, far), out)
-        return out.reshape(32, 128)
-
-    for plane in range(12):
-        slab.g[0][plane + 1, 8:40] = exchange(gathered_ref[pl.ds(plane, 32, stride=32), :])
-    for plane in range(14):
-        slab.b[0][plane, 8:40] = exchange(gathered_ref[pl.ds(plane + 12, 32, stride=32), :])
-
-    slab.clear(14, 32, (0, 13))
-    slab.before(0, 32)
-
-    @pl.loop(1, 13, step=4)
+    for index in range(4):
+        rows = collect[pl.ds(32 * index, 16, stride=2), :]
+        rows = rows + collect[pl.ds(32 * index + 1, 16, stride=2), :]
+        out = out + split_matmul(rows, pair_selector(128, 0, 128, 32 * index, 32))
+    for index in range(16):
+        coarse_ref[index] = out
+
+
+def squeeze_kernel(gathered_ref, out_ref):
+    for row in range(10):
+        value = gathered_ref[pl.ds(row, 16, stride=16), :]
+        for index in range(4):
+            out_ref[index, 16 * row : 16 * row + 16] = value
+
+
+def line_kernel(gathered_ref, out_ref):
+    group = iota((16, 128), 1) >> 5
+    for row in range(10):
+        here = slice(16 * row, 16 * row + 16)
+        pieces = [gathered_ref[position, here] for position in range(4)]
+        for part in range(4):
+            value = pieces[part]
+            for position in range(4):
+                if position != part:
+                    moved = pltpu.roll(pieces[position], (32 * (position - part)) % 128, 1)
+                    value = jnp.where(group == position, moved, value)
+            start = 64 * row + 16 * part
+            out_ref[start : start + 16] = value
+
+
+class Blocks(Level):
+    starts = tuple(32 * block + 8 for block in range(4))
+
+    def __init__(self, refs):
+        super().__init__(refs, 1, True)
+        self.parity = self.lane & 1
+
+    def low(self, row):
+        return row - 32 if row >= self.starts[1] else row + 95
+
+    def high(self, row):
+        return row + 32 if row < self.starts[3] else row - 95
+
+
+def column_kernel(low_ref, own_ref, high_ref, u2_ref, coarse_ref, *scratch):
+    column = Blocks(scratch)
+    at_y = lax.axis_index("gy")
+    low_there = jnp.where(at_y > 0, 1.0, 0.0)
+    high_there = jnp.where(at_y < lax.axis_size("gy") - 1, 1.0, 0.0)
+    (b,), (g,) = column.b, column.g
+
+    def put(target, plane, source, index, scale=None):
+        for block, start in enumerate(column.starts):
+            at = 64 * index + 16 * block
+            value = source[at : at + 16]
+            if scale is not None:
+                value = value * scale
+            target[plane, start : start + 16] = value
+
+    for index in range(4):
+        put(g, 1 + index, low_ref, index, low_there)
+        put(g, 5 + index, own_ref, index)
+        put(g, 9 + index, high_ref, index, high_there)
+        put(b, 5 + index, own_ref, 5 + index)
+    for index in range(5):
+        put(b, index, low_ref, 4 + index, low_there)
+        put(b, 9 + index, high_ref, 5 + index, high_there)
+
+    zero = jnp.zeros((8, 128), F32)
+    for refs in (column.b, column.fy, column.r, column.k):
+        for plane in range(14):
+            refs[0][plane, 24:32] = zero
+            refs[0][plane, 96:104] = zero
+    halves_of = [range(start, start + 16, 8) for start in column.starts]
+    rows = [row for half in halves_of for row in half]
+    for refs in (column.r, column.k):
+        for plane in (0, 13):
+            for row in rows:
+                refs[0][plane, row : row + 8] = zero
+    column.before(0, rows)
+
+    @pl.loop(1, 13, step=2)
     def _(plane):
-        for index in range(4):
-            slab.setup(plane + index, 32, index & 1)
+        for index in range(2):
+            for block, half in enumerate(halves_of):
+                column.setup(plane + index, half, (index + block) & 1)
 
     for step in range(3):
 
         @pl.loop(2 + step, 12 - step, step=2)
         def _(plane):
-            slab.relax(step, plane, 2, range(8, 40, 8))
-
-    for plane in range(4):
-        u2_ref[plane] = slab.k[0][plane + 5, 8:40]
-    for part in range(2):
-        for row in range(8, 40, 8):
-            (first,) = slab.rest(5 + 2 * part, row)
-            (second,) = slab.rest(6 + 2 * part, row)
-            at = slice(32 * part + row - 8, 32 * part + row)
-            rest[at] = 0.5 * (first + second)
-            here = slice(row, row + 8)
-            sums[at] = 0.125 * (slab.b[0][5 + 2 * part, here] + slab.b[0][6 + 2 * part, here])
-    g_rows, b_rows = halves(rest, 32), halves(sums, 32)
-    value = jnp.zeros((32, 128), F32)
-    for part in range(2):
-        own = slice(16 * part, 16 * part + 16)
-        rows = jnp.concatenate([g_rows[own], b_rows[own]], axis=0)
-        value = value + split_matmul(rows, pair_selector(128, 0, 128, 64 * part, 64))
-    for index in range(16):
-        coarse_ref[index] = value
+            column.relax(step, plane, 2, rows)
+
+    at_x = lax.axis_index("gx")
+    for index, start in enumerate(column.starts):
+        for plane in range(4):
+            u2_ref[index, plane : plane + 1] = column.k[0][plane + 5, pl.ds(start + at_x, 1), :]
+        u2_ref[index, 4:8] = jnp.zeros((4, 128), F32)
+
+    halve = [pair_selector(128, 0, 128, 64 * part, 64) for part in range(2)]
+    g_out, b_out = [], []
+    for plane in (5, 7):
+        g_value = jnp.zeros((16, 128), F32)
+        b_value = jnp.zeros((16, 128), F32)
+        for part in range(2):
+            g_parts, b_parts = [], []
+            for offset in (0, 8):
+                g_sum = b_sum = None
+                for block in (2 * part, 2 * part + 1):
+                    row = column.starts[block] + offset
+                    for step in range(2):
+                        (value,) = column.rest(plane, row, step)
+                        weight = b[plane + step, row : row + 8]
+                        g_sum = value if g_sum is None else g_sum + value
+                        b_sum = weight if b_sum is None else b_sum + weight
+                g_parts.append(0.5 * g_sum)
+                b_parts.append(0.125 * b_sum)
+            g_value = g_value + split_matmul(jnp.concatenate(g_parts, axis=0), halve[part])
+            b_value = b_value + split_matmul(jnp.concatenate(b_parts, axis=0), halve[part])
+        g_out.append(g_value)
+        b_out.append(b_value)
+    for index in range(8):
+        for part, value in enumerate(g_out + b_out):
+            coarse_ref[index, 16 * part : 16 * part + 16] = value
 
 
 def coarse_kernel(
     gathered_ref, u0_ref, u1_ref, u2_ref, out_ref,
     r3, rs, k3, ks, inner_3, outer_3, fy3, fz3, d3, ir3, ik3, b3, bs,
     r4, k4, fx4, fy4, fz4, ir4, ik4, g4, b4,
-    pair_3, pair_4, twice_3, twice_2, twice_1, twice_0, level_1,
+    g_rows, b_rows, pair_3, pair_4, twice_3, twice_2, twice_1, twice_0, level_1,
 ):
     at_x = lax.axis_index("gx")
     at_y = lax.axis_index("gy")
@@ -501,6 +557,11 @@
     cell = lane & 63
     parity = ((lane >> 6) + row8 + cell) & 1
     first_half = lane < 64
+    for index in range(8):
+        for part in range(2):
+            rows = pl.ds(2 * index + part, 16, stride=16)
+            g_rows[rows, :] = gathered_ref[index, 16 * part : 16 * part + 16]
+            b_rows[rows, :] = gathered_ref[index, 16 * part + 32 : 16 * part + 48]
     for ref in (r3, rs, k3, ks, b3, bs):
         for plane in (0, 17):
             ref[plane] = jnp.zeros((32, 128), F32)
@@ -509,7 +570,7 @@
             ref[plane, 0:8] = zero
             ref[plane, 24:32] = zero
         for row in (8, 16):
-            value = gathered_ref[plane - 1, row + 8 : row + 16]
+            value = b_rows[16 * plane + row - 24 : 16 * plane + row - 16]
             b3[plane, row : row + 8] = value
             bs[plane, row : row + 8] = pltpu.roll(value, 64, 1)
 
@@ -537,7 +598,7 @@
             d3[plane, here] = total
             ir3[plane, here] = reds
             ik3[plane, here] = jnp.where(inside & (parity == 1), inverse, 0.0)
-            value = gathered_ref[plane - 1, row - 8 : row] * reds
+            value = g_rows[16 * plane + row - 24 : 16 * plane + row - 16] * reds
             r3[plane, here] = value
             rs[plane, here] = pltpu.roll(value, 64, 1)
 
@@ -548,7 +609,8 @@
         along_x = along_x + outer_3[plane, here] * outer(swapped, plane, here)
         along_y = fy3[plane, here] * ref[plane, high] + fy3[plane, low] * ref[plane, low]
         along_z = face * pltpu.roll(v, 127, 1) + pltpu.roll(face * v, 1, 1)
-        return (gathered_ref[plane - 1, row - 8 : row] + along_x) + (along_y + along_z)
+        g = g_rows[16 * plane + row - 24 : 16 * plane + row - 16]
+        return (g + along_x) + (along_y + along_z)
 
     for step in range(3):
         source, inverse, target = (
@@ -635,9 +697,8 @@
         twice_2[pl.ds(1, 8, stride=2), :] = fine
         for index in range(2):
             own = u2_ref[2 * part + index]
-            own = pltpu.roll(own, lax.rem(32 - 4 * at_y, 32), 0)
             own = pltpu.roll(own, lax.rem(128 - 32 * at_z, 128), 1)
-            level_2.append(own[0:8] + twice_2[0:8])
+            level_2.append(own + twice_2[0:8])
     fine = split_matmul(jnp.concatenate(level_2, axis=0), spread_selector(0, 0, 32))
     twice_1[pl.ds(0, 32, stride=2), :] = fine
     twice_1[pl.ds(1, 32, stride=2), :] = fine
@@ -702,7 +763,7 @@
     u0, u1, coarse = call(
         fine_kernel,
         40,
-        [(BLOCK, BLOCK, 128), (8, 8, 128), (16, 128)],
+        [(BLOCK, BLOCK, 128), (8, 8, 128), (16, 16, 128)],
         Level.scratch(2, B_PLANES, ROWS)
         + Level.scratch(1, 20, 24)
         + [(512, 128)] * 2
@@ -711,18 +772,20 @@
         low, high, main, after, before,
     )
 
-    low, high = shift(coarse, "gx", 1), shift(coarse, "gx", -1)
-    (slab,) = call(spread_kernel, 2, [(32, 32, 128)], [(32, 128)], low, coarse, high)
-    slab = lax.all_to_all(slab, ("gy", "gz"), 0, 0, tiled=True)
+    column = lax.all_to_all(coarse, "gx", 0, 0, tiled=True)
+    (column,) = call(squeeze_kernel, 2, [(4, 160, 128)], [], column.reshape(256, 128))
+    column = lax.all_to_all(column, "gz", 0, 0, tiled=True)
+    (column,) = call(line_kernel, 2, [(640, 128)], [], column)
+    low, high = around(column, "gy", 1), around(column, "gy", -1)
     u2, coarse = call(
-        slab_kernel,
-        8,
-        [(4, 32, 128), (16, 32, 128)],
-        Level.scratch(1, 14, 32) + [(64, 128)] * 2,
-        slab.reshape(1024, 128),
+        column_kernel,
+        13,
+        [(4, 8, 128), (8, 64, 128)],
+        Level.scratch(1, 14, 112),
+        low, column, high,
     )
 
-    whole = lax.all_to_all(coarse, "gx", 0, 0, tiled=True)
+    whole = lax.all_to_all(coarse, "gy", 0, 0, tiled=True)
     (out,) = call(
         coarse_kernel,
         8,
@@ -730,7 +793,7 @@
         [(18, 32, 128)] * 13
         + [(18, 8, 128)] * 7
         + [(16, 8, 128), (18, 8, 128)]
-        + [(256, 128)] * 2
+        + [(256, 128)] * 4
         + [(16, 128), (16, 128), (64, 128), (128, 128), (64, 128)],
         whole, u0, u1, u2,
     )

time: 114 us -> 113 us (level)
  waiting for transfers between devices: 15 us -> 20.2 us
  starting transfers between devices: 22.8 us -> 18.3 us
  blocking collectives: 55.6 us -> 53.3 us
    ppermute x2 -> x4, waiting for transfers between devices: 6.42 us -> 14.1 us  [around(): lax.ppermute(value, axis, [(i, (i + step) % count) for i in range(count)])]
    ppermute x4 -> x2, starting transfers between devices: 15.8 us -> 8.8 us  [shift(): return lax.ppermute(value, axis, pairs)]
    ppermute x2 -> x4, starting transfers between devices: 2.96 us -> 5.43 us  [around(): lax.ppermute(value, axis, [(i, (i + step) % count) for i in range(count)])]
    ppermute x4 -> x2, waiting for transfers between devices: 6.21 us -> 3.77 us  [shift(): return lax.ppermute(value, axis, pairs)]
    all_to_all x2 -> x3, blocking collectives: 55.6 us -> 53.3 us  [the longest x1 29.1 us: on_device(): column = lax.all_to_all(coarse, 'gx', 0, 0, tiled=True)]
    pallas_call x6 -> x7, Pallas kernels: 19.4 us -> 19.9 us  [call(): pl.pallas_call(kernel, out_shape=[jax.ShapeDtypeStruct(shape, F32) for sh...]
  transfers between devices with their start and end apart: 8 -> 8, of which waited for: 5 -> 6; matrix products, arithmetic and copies ran while one was open for 0% -> 0% of each run, Pallas kernels for 0% -> 0%
where the time goes in v3:
time: 113 us
  blocking collectives  53.3 us (47%)
  waiting for transfers between devices  20.2 us (18%)
  Pallas kernels  19.9 us (18%)
  starting transfers between devices  18.3 us (16%)
    all_to_all x1, blocking collectives, on_device(): column = lax.all_to_all(coarse, 'gx', 0, 0, tiled=True)  29.1 us
    pallas_call x7, Pallas kernels, call(): pl.pallas_call(kernel, out_shape=[jax.ShapeDtypeStruct(shape, F32) for sh...  19.9 us
    all_to_all x1, blocking collectives, on_device(): column = lax.all_to_all(column, 'gz', 0, 0, tiled=True)  14.2 us
    ppermute x4, waiting for transfers between devices, around(): lax.ppermute(value, axis, [(i, (i + step) % count) for i in range(count)])  14.1 us
    all_to_all x1, blocking collectives, on_device(): whole = lax.all_to_all(coarse, 'gy', 0, 0, tiled=True)  9.92 us
    ppermute x2, starting transfers between devices, shift(): return lax.ppermute(value, axis, pairs)  8.8 us
    ppermute x4, starting transfers between devices, around(): lax.ppermute(value, axis, [(i, (i + step) % count) for i in range(count)])  5.43 us
    ppermute x2, starting transfers between devices, swap(): return lax.ppermute(value, axis, pairs)  4.07 us
  transfers between devices with their start and end apart: 8, of which 6 were waited for; matrix products, arithmetic and copies ran while one was open for 0% of the time, Pallas kernels for 0%

profile of v3, /device:TPU:32, one launch (start us, length us, event | category | flops | bytes accessed | tf_op | source)
XLA Modules:
  0.0 112.9 jit_solution(10440409852422313134)
XLA Ops:
  0.0 0.0 copy-start
  0.0 1.0 fusion
  1.0 0.0 copy-done
  1.1 3.8 %collective-permute-start = (f32[25,16,128]{2,1,0:T(8,128)S(1)}, f32[25,16,128]{2,1,0:T(8,128)S(1)}, u32[]{:S(2)}, u32[]{:S(2)}) collective-permute-start(f32[25,16,128]{2,1,0:T(8,128)S(1)} %pad_maximum_fusion), channel_id=1, source_target_pairs={{0,32},{32,64},{64,96},{96,128},{128,160},{160,192},{192,224},{224... | collective-permute-start | bytes 614408 | tf_op jit(solution)/shard_map/ppermute | solution.py:731
  4.9 0.0 copy-start.1
  4.9 5.0 %collective-permute-start.1 = (f32[25,16,128]{2,1,0:T(8,128)S(1)}, f32[25,16,128]{2,1,0:T(8,128)S(1)}, u32[]{:S(2)}, u32[]{:S(2)}) collective-permute-start(f32[25,16,128]{2,1,0:T(8,128)S(1)} %pad_maximum_fusion.1), channel_id=1, source_target_pairs={{32,0},{64,32},{96,64},{128,96},{160,128},{192,160},{224,192},{256... | collective-permute-start | bytes 614408 | tf_op jit(solution)/shard_map/ppermute | solution.py:731
  9.9 1.6 %collective-permute-done.low_ref = f32[25,16,128]{2,1,0:T(8,128)S(1)} collective-permute-done((f32[25,16,128]{2,1,0:T(8,128)S(1)}, f32[25,16,128]{2,1,0:T(8,128)S(1)}, u32[]{:S(2)}, u32[]{:S(2)}) %collective-permute-start) | collective-permute-done | bytes 204832 | tf_op jit(solution)/shard_map/ppermute | solution.py:731
  11.5 2.1 %collective-permute-done.1.high_ref = f32[25,16,128]{2,1,0:T(8,128)S(1)} collective-permute-done((f32[25,16,128]{2,1,0:T(8,128)S(1)}, f32[25,16,128]{2,1,0:T(8,128)S(1)}, u32[]{:S(2)}, u32[]{:S(2)}) %collective-permute-start.1) | collective-permute-done | bytes 204832 | tf_op jit(solution)/shard_map/ppermute | solution.py:731
  13.7 0.0 copy-done.1
  13.7 0.2 shard_map.28
  13.9 3.4 %collective-permute-start.2 = (f32[11,16,128]{2,1,0:T(8,128)S(1)}, f32[11,16,128]{2,1,0:T(8,128)S(1)}, u32[]{:S(2)}, u32[]{:S(2)}) collective-permute-start(f32[11,16,128]{2,1,0:T(8,128)S(1)} %get-tuple-element.21), channel_id=1, source_target_pairs={{0,1},{2,3},{1,0},{3,2},{4,5},{6,7},{5,4},{7,6},{8,9},{10,11},{9,8... | collective-permute-start | bytes 270344 | tf_op jit(solution)/shard_map/ppermute | solution.py:743
  17.3 0.7 collective-permute-start.3
  18.0 2.3 %collective-permute-done.2.first_ref = f32[11,16,128]{2,1,0:T(8,128)S(1)} collective-permute-done((f32[11,16,128]{2,1,0:T(8,128)S(1)}, f32[11,16,128]{2,1,0:T(8,128)S(1)}, u32[]{:S(2)}, u32[]{:S(2)}) %collective-permute-start.2) | collective-permute-done | bytes 90144 | tf_op jit(solution)/shard_map/ppermute | solution.py:743
  20.3 0.0 collective-permute-done.3.second_ref
  20.3 0.1 shard_map.29
  20.4 0.0 collective-permute-start.4
  20.5 2.9 %collective-permute-start.5 = (f32[944,128]{1,0:T(8,128)S(1)}, f32[944,128]{1,0:T(8,128)S(1)}, u32[]{:S(2)}, u32[]{:S(2)}) collective-permute-start(f32[944,128]{1,0:T(8,128)S(1)} %get-tuple-element.24), channel_id=1, source_target_pairs={{0,28},{4,0},{8,4},{12,8},{16,12},{20,16},{24,20},{28,24},{1,29},{... | collective-permute-start | bytes 1449992 | tf_op jit(solution)/shard_map/ppermute | solution.py:736
  23.4 6.4 %collective-permute-done.4.low_ref = f32[944,128]{1,0:T(8,128)S(1)} collective-permute-done((f32[944,128]{1,0:T(8,128)S(1)}, f32[944,128]{1,0:T(8,128)S(1)}, u32[]{:S(2)}, u32[]{:S(2)}) %collective-permute-start.4) | collective-permute-done | bytes 483360 | tf_op jit(solution)/shard_map/ppermute | solution.py:736
  29.8 0.0 collective-permute-done.5.high_ref
  29.8 12.3 %shard_map.30 = (f32[16,16,128]{2,1,0:T(8,128)S(1)}, f32[8,8,128]{2,1,0:T(8,128)S(1)}, f32[16,16,128]{2,1,0:T(8,128)S(1)}) custom-call(f32[944,128]{1,0:T(8,128)S(1)} %collective-permute-done.4.low_ref, f32[944,128]{1,0:T(8,128)S(1)} %collective-permute-done.5.high_ref, f32[82,16,128]{2,1,0:T(8,128)S(1)} %get-tuple-element.25.main_ref, ...), custom_call_target="tpu_custom_call" | custom-call | tf_op jit(solution)/shard_map/pallas_call | solution.py:718
  42.1 29.1 %all_to_all.15 = f32[16,16,128]{2,1,0:T(8,128)S(1)} all-to-all(f32[16,16,128]{2,1,0:T(8,128)S(1)} %get-tuple-element.28), channel_id=1, replica_groups=mesh['gx'=16,'gy'=8,'gz'=4] {'gx'}, dimensions={0} | all-to-all | bytes 262144 | tf_op jit(solution)/shard_map/all_to_all | solution.py:775
  71.3 14.2 %all_to_all.16.gathered_ref = f32[4,160,128]{2,1,0:T(8,128)S(1)} all-to-all(f32[4,160,128]{2,1,0:T(8,128)S(1)} %shard_map.31), channel_id=1, replica_groups=mesh['gx'=16,'gy'=8,'gz'=4] {'gz'}, dimensions={0} | all-to-all | bytes 655360 | tf_op jit(solution)/shard_map/all_to_all | solution.py:777
  85.5 0.3 shard_map.32.own_ref
  85.8 2.5 %collective-permute-start.7 = (f32[640,128]{1,0:T(8,128)S(1)}, f32[640,128]{1,0:T(8,128)S(1)}, u32[]{:S(2)}, u32[]{:S(2)}) collective-permute-start(f32[640,128]{1,0:T(8,128)S(1)} %shard_map.32.own_ref), channel_id=1, source_target_pairs={{0,28},{4,0},{8,4},{12,8},{16,12},{20,16},{24,20},{28,24},{1,29},{... | collective-permute-start | bytes 983048 | tf_op jit(solution)/shard_map/ppermute | solution.py:736
  88.3 0.0 collective-permute-start.6
  88.3 4.6 %collective-permute-done.7.high_ref = f32[640,128]{1,0:T(8,128)S(1)} collective-permute-done((f32[640,128]{1,0:T(8,128)S(1)}, f32[640,128]{1,0:T(8,128)S(1)}, u32[]{:S(2)}, u32[]{:S(2)}) %collective-permute-start.7) | collective-permute-done | bytes 327712 | tf_op jit(solution)/shard_map/ppermute | solution.py:736
  92.9 3.1 %collective-permute-done.6.low_ref = f32[640,128]{1,0:T(8,128)S(1)} collective-permute-done((f32[640,128]{1,0:T(8,128)S(1)}, f32[640,128]{1,0:T(8,128)S(1)}, u32[]{:S(2)}, u32[]{:S(2)}) %collective-permute-start.6) | collective-permute-done | bytes 327712 | tf_op jit(solution)/shard_map/ppermute | solution.py:736
  96.0 2.4 %shard_map.33 = (f32[4,8,128]{2,1,0:T(8,128)S(1)}, f32[8,64,128]{2,1,0:T(8,128)S(1)}) custom-call(f32[640,128]{1,0:T(8,128)S(1)} %collective-permute-done.6.low_ref, f32[640,128]{1,0:T(8,128)S(1)} %shard_map.32.own_ref, f32[640,128]{1,0:T(8,128)S(1)} %collective-permute-done.7.high_ref), custom_call_target="tpu_custom_call" | custom-call | tf_op jit(solution)/shard_map/pallas_call | solution.py:718
  98.4 9.9 %all_to_all.17.gathered_ref = f32[8,64,128]{2,1,0:T(8,128)S(1)} all-to-all(f32[8,64,128]{2,1,0:T(8,128)S(1)} %get-tuple-element.29), channel_id=1, replica_groups=mesh['gx'=16,'gy'=8,'gz'=4] {'gy'}, dimensions={0} | all-to-all | bytes 524288 | tf_op jit(solution)/shard_map/all_to_all | solution.py:788
  108.4 4.5 %shard_map.34 = f32[16,16,128]{2,1,0:T(8,128)} custom-call(f32[8,64,128]{2,1,0:T(8,128)S(1)} %all_to_all.17.gathered_ref, f32[16,16,128]{2,1,0:T(8,128)S(1)} %get-tuple-element.30.u0_ref, f32[8,8,128]{2,1,0:T(8,128)S(1)} %get-tuple-element.31.u1_ref, f32[4,8,128]{2,1,0:T(8,128)S(1)} %get-tuple-element.32.u2_ref), custom_call_target="tpu_custom_call" | custom-call | tf_op jit(solution)/shard_map/pallas_call | solution.py:718
  (4 shorter events, 0.1 us)
Async XLA Ops:
  0.0 1.0 copy-start
  1.1 10.5 %collective-permute-start = (f32[25,16,128]{2,1,0:T(8,128)S(1)}, f32[25,16,128]{2,1,0:T(8,128)S(1)}, u32[]{:S(2)}, u32[]{:S(2)}) collective-permute-start(f32[25,16,128]{2,1,0:T(8,128)S(1)} %pad_maximum_fusion), channel_id=1, source_target_pairs={{0,32},{32,64},{64,96},{96,128},{128,160},{160,192},{192,224},{224... | collective-permute-start | bytes 614408 | tf_op jit(solution)/shard_map/ppermute | solution.py:731
  4.9 8.8 %copy-start.1 = (f32[16,16,128]{2,1,0:T(8,128)S(1)}, f32[16,16,128]{2,1,0:T(8,128)}, u32[]{:S(2)}) copy-start(f32[16,16,128]{2,1,0:T(8,128)} %f_ref.1) | copy-start | bytes 393220
  4.9 8.7 %collective-permute-start.1 = (f32[25,16,128]{2,1,0:T(8,128)S(1)}, f32[25,16,128]{2,1,0:T(8,128)S(1)}, u32[]{:S(2)}, u32[]{:S(2)}) collective-permute-start(f32[25,16,128]{2,1,0:T(8,128)S(1)} %pad_maximum_fusion.1), channel_id=1, source_target_pairs={{32,0},{64,32},{96,64},{128,96},{160,128},{192,160},{224,192},{256... | collective-permute-start | bytes 614408 | tf_op jit(solution)/shard_map/ppermute | solution.py:731
  13.9 6.4 %collective-permute-start.2 = (f32[11,16,128]{2,1,0:T(8,128)S(1)}, f32[11,16,128]{2,1,0:T(8,128)S(1)}, u32[]{:S(2)}, u32[]{:S(2)}) collective-permute-start(f32[11,16,128]{2,1,0:T(8,128)S(1)} %get-tuple-element.21), channel_id=1, source_target_pairs={{0,1},{2,3},{1,0},{3,2},{4,5},{6,7},{5,4},{7,6},{8,9},{10,11},{9,8... | collective-permute-start | bytes 270344 | tf_op jit(solution)/shard_map/ppermute | solution.py:743
  17.3 3.0 %collective-permute-start.3 = (f32[11,16,128]{2,1,0:T(8,128)S(1)}, f32[11,16,128]{2,1,0:T(8,128)S(1)}, u32[]{:S(2)}, u32[]{:S(2)}) collective-permute-start(f32[11,16,128]{2,1,0:T(8,128)S(1)} %get-tuple-element.22), channel_id=1, source_target_pairs={{1,2},{2,1},{5,6},{6,5},{9,10},{10,9},{13,14},{14,13},{17,18},{18,... | collective-permute-start | bytes 270344 | tf_op jit(solution)/shard_map/ppermute | solution.py:743
  20.4 9.4 %collective-permute-start.4 = (f32[944,128]{1,0:T(8,128)S(1)}, f32[944,128]{1,0:T(8,128)S(1)}, u32[]{:S(2)}, u32[]{:S(2)}) collective-permute-start(f32[944,128]{1,0:T(8,128)S(1)} %get-tuple-element.23), channel_id=1, source_target_pairs={{0,4},{4,8},{8,12},{12,16},{16,20},{20,24},{24,28},{28,0},{1,5},{5... | collective-permute-start | bytes 1449992 | tf_op jit(solution)/shard_map/ppermute | solution.py:736
  20.5 9.4 %collective-permute-start.5 = (f32[944,128]{1,0:T(8,128)S(1)}, f32[944,128]{1,0:T(8,128)S(1)}, u32[]{:S(2)}, u32[]{:S(2)}) collective-permute-start(f32[944,128]{1,0:T(8,128)S(1)} %get-tuple-element.24), channel_id=1, source_target_pairs={{0,28},{4,0},{8,4},{12,8},{16,12},{20,16},{24,20},{28,24},{1,29},{... | collective-permute-start | bytes 1449992 | tf_op jit(solution)/shard_map/ppermute | solution.py:736
  85.8 7.1 %collective-permute-start.7 = (f32[640,128]{1,0:T(8,128)S(1)}, f32[640,128]{1,0:T(8,128)S(1)}, u32[]{:S(2)}, u32[]{:S(2)}) collective-permute-start(f32[640,128]{1,0:T(8,128)S(1)} %shard_map.32.own_ref), channel_id=1, source_target_pairs={{0,28},{4,0},{8,4},{12,8},{16,12},{20,16},{24,20},{28,24},{1,29},{... | collective-permute-start | bytes 983048 | tf_op jit(solution)/shard_map/ppermute | solution.py:736
  88.3 7.7 %collective-permute-start.6 = (f32[640,128]{1,0:T(8,128)S(1)}, f32[640,128]{1,0:T(8,128)S(1)}, u32[]{:S(2)}, u32[]{:S(2)}) collective-permute-start(f32[640,128]{1,0:T(8,128)S(1)} %shard_map.32.own_ref), channel_id=1, source_target_pairs={{0,4},{4,8},{8,12},{12,16},{16,20},{20,24},{24,28},{28,0},{1,5},{5... | collective-permute-start | bytes 983048 | tf_op jit(solution)/shard_map/ppermute | solution.py:736

commit v4 on v3

--- a/solution.py
+++ b/solution.py
@@ -155,32 +155,47 @@
                 self.r[column][here] = g[column] * reds
                 self.k[column][here] = jnp.zeros((8, 128), F32)
 
-    def total(self, source, base, step, row, held=None):
-        held = {} if held is None else held
-
-        def load(ref, plane):
-            key = (id(ref), plane)
-            if key not in held:
-                held[key] = ref[base + plane, row : row + 8]
-            return held[key]
-
-        v = [load(ref, step) for ref in source]
-        face_z = [load(ref, step) for ref in self.fz]
-        z_high = self.turn(v, 1)
-        z_low = self.turn([face * value for face, value in zip(face_z, v)], -1)
+    def load(self, ref, base, step, row, held):
+        key = (id(ref), id(base), step)
+        if key not in held:
+            held[key] = ref[base + step, row : row + 8]
+        return held[key]
+
+    def along_z(self, source, places, row, held):
+        fields, scaled = [], []
+        for base, step in places:
+            v = [self.load(ref, base, step, row, held) for ref in source]
+            face = [self.load(ref, base, step, row, held) for ref in self.fz]
+            fields.append((v, face))
+            scaled.append([a * b for a, b in zip(face, v)])
+        v_sum, w_sum = fields[0][0], scaled[0]
+        for (v, _), w in zip(fields[1:], scaled[1:]):
+            v_sum = [a + b for a, b in zip(v_sum, v)]
+            w_sum = [a + b for a, b in zip(w_sum, w)]
+        high, low = self.turn(v_sum, 1), self.turn(w_sum, -1)
+        return [[f * h + l for f, h, l in zip(face, high, low)] for _, face in fields]
+
+    def total(self, source, base, step, row, held, along_z):
         out = []
         for column in range(self.columns):
             ref, fx, fy = source[column], self.fx[column], self.fy[column]
-            along_x = load(fx, step) * load(ref, step + 1) + load(fx, step - 1) * load(ref, step - 1)
+            along_x = self.load(fx, base, step, row, held) * self.load(
+                ref, base, step + 1, row, held
+            ) + self.load(fx, base, step - 1, row, held) * self.load(
+                ref, base, step - 1, row, held
+            )
             low = slice(self.low(row), self.low(row) + 8)
             high = slice(self.high(row), self.high(row) + 8)
             plane = base + step
-            along_y = load(fy, step) * ref[plane, high] + fy[plane, low] * ref[plane, low]
-            along_z = face_z[column] * z_high[column] + z_low[column]
-            out.append((load(self.g[column], step) + along_x) + (along_y + along_z))
+            along_y = (
+                self.load(fy, base, step, row, held) * ref[plane, high]
+                + fy[plane, low] * ref[plane, low]
+            )
+            g = self.load(self.g[column], base, step, row, held)
+            out.append((g + along_x) + (along_y + along_z[column]))
         return out
 
-    def relax(self, step, base, count, rows):
+    def relax(self, step, pairs, rows):
         source, inverse, target = (
             (self.r, self.ik, self.k),
             (self.k, self.ir, self.r),
@@ -188,17 +203,25 @@
         )[step]
         for row in rows:
             held = {}
-            for index in range(count):
-                values = self.total(source, base, index, row, held)
-                scale = self.at(inverse, base + index, row)
-                values = [value * factor for value, factor in zip(values, scale)]
-                if step == 2:
-                    own = self.at(self.r, base + index, row)
-                    values = [a + b for a, b in zip(values, own)]
-                self.put(target, base + index, row, values)
+            for places in pairs:
+                sums = self.along_z(source, places, row, held)
+                for (base, index), along_z in zip(places, sums):
+                    values = self.total(source, base, index, row, held, along_z)
+                    scale = self.at(inverse, base + index, row)
+                    values = [value * factor for value, factor in zip(values, scale)]
+                    if step == 2:
+                        own = self.at(self.r, base + index, row)
+                        values = [a + b for a, b in zip(values, own)]
+                    self.put(target, base + index, row, values)
+
+    @staticmethod
+    def adjacent(base, count):
+        return [((base, index), (base, index + 1)) for index in range(0, count, 2)]
 
     def rest(self, base, row, step=0, held=None):
-        values = self.total(self.k, base, step, row, held)
+        held = {} if held is None else held
+        (along_z,) = self.along_z(self.k, ((base, step),), row, held)
+        values = self.total(self.k, base, step, row, held, along_z)
         plane = base + step
         out = []
         for column, value in enumerate(values):
@@ -210,6 +233,13 @@
 
 def halves(ref, rows):
     return ref[pl.ds(0, rows, stride=2), :] + ref[pl.ds(1, rows, stride=2), :]
+
+
+def edge_kernel(f_ref, b_ref, upper_ref, lower_ref):
+    upper_ref[0:F_HALO] = f_ref[BLOCK - F_HALO : BLOCK]
+    upper_ref[F_HALO:] = b_ref[BLOCK - B_HALO : BLOCK]
+    lower_ref[0:F_HALO] = f_ref[0:F_HALO]
+    lower_ref[F_HALO:] = b_ref[0:B_HALO]
 
 
 def pack_kernel(
@@ -343,16 +373,16 @@
         beside = 2 - step
         near = B_HALO - beside
 
-        count = (4, 3, 4)[step]
-
-        @pl.loop(near, near + BLOCK + 2 * beside, step=count)
+
+        @pl.loop(near, near + BLOCK + 2 * beside, step=2)
         def _(plane):
-            fine.relax(step, plane, count, every)
+            fine.relax(step, fine.adjacent(plane, 2), every)
 
         @pl.loop(near - 9, near, step=3)
         def _(plane):
-            fine.relax(step, plane, 3, inner)
-            fine.relax(step, plane + BLOCK + 2 * beside + 9, 3, inner)
+            other = plane + BLOCK + 2 * beside + 9
+            for base in (plane, other):
+                fine.relax(step, [((base, index),) for index in range(3)], inner)
 
     for plane in range(BLOCK):
         u0_ref[plane] = fine.k[0][plane + B_HALO, 8 + BLOCK : 8 + 2 * BLOCK]
@@ -402,7 +432,7 @@
 
         @pl.loop(2, 18, step=4)
         def _(plane):
-            middle.relax(step, plane, 4, range(8, 32, 8))
+            middle.relax(step, middle.adjacent(plane, 4), range(8, 32, 8))
 
     for plane in range(8):
         u1_ref[plane] = middle.k[0][plane + 6, 16:24]
@@ -506,7 +536,7 @@
 
         @pl.loop(2 + step, 12 - step, step=2)
         def _(plane):
-            column.relax(step, plane, 2, rows)
+            column.relax(step, column.adjacent(plane, 2), rows)
 
     at_x = lax.axis_index("gx")
     for index, start in enumerate(column.starts):
@@ -665,14 +695,19 @@
         r4[plane] = g4[plane - 1] * reds
 
     def half_4(source, inverse, target):
-        for plane in range(1, 17):
-            v = source[plane]
-            face_y, face_z = fy4[plane], fz4[plane]
-            along_x = fx4[plane] * source[plane + 1] + fx4[plane - 1] * source[plane - 1]
-            along_y = face_y * pltpu.roll(v, 7, 0) + pltpu.roll(face_y * v, 1, 0)
-            along_z = face_z * pltpu.roll(v, 127, 1) + pltpu.roll(face_z * v, 1, 1)
-            value = (g4[plane - 1] + along_x) + (along_y + along_z)
-            target[plane] = value * inverse[plane]
+        for first in range(1, 17, 2):
+            pair = (first, first + 1)
+            v = source[first] + source[first + 1]
+            y_face = fy4[first] * source[first] + fy4[first + 1] * source[first + 1]
+            z_face = fz4[first] * source[first] + fz4[first + 1] * source[first + 1]
+            y_high, y_low = pltpu.roll(v, 7, 0), pltpu.roll(y_face, 1, 0)
+            z_high, z_low = pltpu.roll(v, 127, 1), pltpu.roll(z_face, 1, 1)
+            for plane in pair:
+                along_x = fx4[plane] * source[plane + 1] + fx4[plane - 1] * source[plane - 1]
+                along_y = fy4[plane] * y_high + y_low
+                along_z = fz4[plane] * z_high + z_low
+                value = (g4[plane - 1] + along_x) + (along_y + along_z)
+                target[plane] = value * inverse[plane]
 
     half_4(r4, ik4, k4)
 
@@ -745,8 +780,8 @@
 
 def on_device(right_side, conductivity):
     f, b = right_side, conductivity
-    upper = jnp.concatenate([f[BLOCK - F_HALO :], b[BLOCK - B_HALO :]], axis=0)
-    lower = jnp.concatenate([f[:F_HALO], b[:B_HALO]], axis=0)
+    edge = (F_HALO + B_HALO, BLOCK, 128)
+    upper, lower = call(edge_kernel, 2, [edge, edge], [], f, b)
     low, high = shift(upper, "gx", 1), shift(lower, "gx", -1)
 
     strip = (GROUPS, BLOCK, 128)

time: 113 us -> 113 us (level)
    unnamed x4 -> x8, local copies, waits for them, and re-layouts: 0.01 us -> 1.81 us
    pallas_call x7 -> x8, Pallas kernels: 19.9 us -> 18.8 us  [call(): pl.pallas_call(kernel, out_shape=[jax.ShapeDtypeStruct(shape, F32) for sh...]
where the time goes in v4:
time: 113 us
  blocking collectives  53.3 us (47%)
  waiting for transfers between devices  20.2 us (18%)
  Pallas kernels  18.8 us (17%)
  starting transfers between devices  18.3 us (16%)
  local copies, waits for them, and re-layouts  1.81 us (2%)
    all_to_all x1, blocking collectives, on_device(): column = lax.all_to_all(coarse, 'gx', 0, 0, tiled=True)  29.1 us
    pallas_call x8, Pallas kernels, call(): pl.pallas_call(kernel, out_shape=[jax.ShapeDtypeStruct(shape, F32) for sh...  18.8 us
    all_to_all x1, blocking collectives, on_device(): column = lax.all_to_all(column, 'gz', 0, 0, tiled=True)  14.2 us
    ppermute x4, waiting for transfers between devices, around(): lax.ppermute(value, axis, [(i, (i + step) % count) for i in range(count)])  14.1 us
    all_to_all x1, blocking collectives, on_device(): whole = lax.all_to_all(coarse, 'gy', 0, 0, tiled=True)  9.92 us
    ppermute x2, starting transfers between devices, shift(): return lax.ppermute(value, axis, pairs)  8.8 us
    ppermute x4, starting transfers between devices, around(): lax.ppermute(value, axis, [(i, (i + step) % count) for i in range(count)])  5.43 us
    ppermute x2, starting transfers between devices, swap(): return lax.ppermute(value, axis, pairs)  4.07 us
  transfers between devices with their start and end apart: 8, of which 6 were waited for; matrix products, arithmetic and copies ran while one was open for 0% of the time, Pallas kernels for 0%

profile of v4, /device:TPU:32, one launch (start us, length us, event | category | flops | bytes accessed | tf_op | source)
XLA Modules:
  0.0 112.5 jit_solution(2443146704148029283)
XLA Ops:
  0.0 0.0 copy-start
  0.0 0.9 copy-done
  0.9 0.0 copy-start.2
  0.9 0.9 copy-done.2
  1.8 0.0 copy-start.1
  1.8 4.0 %collective-permute-start = (f32[25,16,128]{2,1,0:T(8,128)S(1)}, f32[25,16,128]{2,1,0:T(8,128)S(1)}, u32[]{:S(2)}, u32[]{:S(2)}) collective-permute-start(f32[25,16,128]{2,1,0:T(8,128)S(1)} %get-tuple-element.21), channel_id=1, source_target_pairs={{0,32},{32,64},{64,96},{96,128},{128,160},{160,192},{192,224},{224... | collective-permute-start | bytes 614408 | tf_op jit(solution)/shard_map/ppermute | solution.py:766
  5.8 4.8 %collective-permute-start.1 = (f32[25,16,128]{2,1,0:T(8,128)S(1)}, f32[25,16,128]{2,1,0:T(8,128)S(1)}, u32[]{:S(2)}, u32[]{:S(2)}) collective-permute-start(f32[25,16,128]{2,1,0:T(8,128)S(1)} %get-tuple-element.22), channel_id=1, source_target_pairs={{32,0},{64,32},{96,64},{128,96},{160,128},{192,160},{224,192},{256... | collective-permute-start | bytes 614408 | tf_op jit(solution)/shard_map/ppermute | solution.py:766
  10.7 1.8 %collective-permute-done.low_ref = f32[25,16,128]{2,1,0:T(8,128)S(1)} collective-permute-done((f32[25,16,128]{2,1,0:T(8,128)S(1)}, f32[25,16,128]{2,1,0:T(8,128)S(1)}, u32[]{:S(2)}, u32[]{:S(2)}) %collective-permute-start) | collective-permute-done | bytes 204832 | tf_op jit(solution)/shard_map/ppermute | solution.py:766
  12.4 2.0 %collective-permute-done.1.high_ref = f32[25,16,128]{2,1,0:T(8,128)S(1)} collective-permute-done((f32[25,16,128]{2,1,0:T(8,128)S(1)}, f32[25,16,128]{2,1,0:T(8,128)S(1)}, u32[]{:S(2)}, u32[]{:S(2)}) %collective-permute-start.1) | collective-permute-done | bytes 204832 | tf_op jit(solution)/shard_map/ppermute | solution.py:766
  14.4 0.0 copy-done.1
  14.4 0.0 copy-done.3
  14.4 0.2 shard_map.29
  14.7 3.4 %collective-permute-start.2 = (f32[11,16,128]{2,1,0:T(8,128)S(1)}, f32[11,16,128]{2,1,0:T(8,128)S(1)}, u32[]{:S(2)}, u32[]{:S(2)}) collective-permute-start(f32[11,16,128]{2,1,0:T(8,128)S(1)} %get-tuple-element.25), channel_id=1, source_target_pairs={{0,1},{2,3},{1,0},{3,2},{4,5},{6,7},{5,4},{7,6},{8,9},{10,11},{9,8... | collective-permute-start | bytes 270344 | tf_op jit(solution)/shard_map/ppermute | solution.py:778
  18.1 0.7 collective-permute-start.3
  18.8 2.3 %collective-permute-done.2.first_ref = f32[11,16,128]{2,1,0:T(8,128)S(1)} collective-permute-done((f32[11,16,128]{2,1,0:T(8,128)S(1)}, f32[11,16,128]{2,1,0:T(8,128)S(1)}, u32[]{:S(2)}, u32[]{:S(2)}) %collective-permute-start.2) | collective-permute-done | bytes 90144 | tf_op jit(solution)/shard_map/ppermute | solution.py:778
  21.1 0.0 collective-permute-done.3.second_ref
  21.1 0.1 shard_map.30
  21.2 0.0 collective-permute-start.4
  21.2 2.9 %collective-permute-start.5 = (f32[944,128]{1,0:T(8,128)S(1)}, f32[944,128]{1,0:T(8,128)S(1)}, u32[]{:S(2)}, u32[]{:S(2)}) collective-permute-start(f32[944,128]{1,0:T(8,128)S(1)} %get-tuple-element.28), channel_id=1, source_target_pairs={{0,28},{4,0},{8,4},{12,8},{16,12},{20,16},{24,20},{28,24},{1,29},{... | collective-permute-start | bytes 1449992 | tf_op jit(solution)/shard_map/ppermute | solution.py:771
  24.2 6.4 %collective-permute-done.4.low_ref = f32[944,128]{1,0:T(8,128)S(1)} collective-permute-done((f32[944,128]{1,0:T(8,128)S(1)}, f32[944,128]{1,0:T(8,128)S(1)}, u32[]{:S(2)}, u32[]{:S(2)}) %collective-permute-start.4) | collective-permute-done | bytes 483360 | tf_op jit(solution)/shard_map/ppermute | solution.py:771
  30.6 0.0 collective-permute-done.5.high_ref
  30.6 12.1 %shard_map.31 = (f32[16,16,128]{2,1,0:T(8,128)S(1)}, f32[8,8,128]{2,1,0:T(8,128)S(1)}, f32[16,16,128]{2,1,0:T(8,128)S(1)}) custom-call(f32[944,128]{1,0:T(8,128)S(1)} %collective-permute-done.4.low_ref, f32[944,128]{1,0:T(8,128)S(1)} %collective-permute-done.5.high_ref, f32[82,16,128]{2,1,0:T(8,128)S(1)} %get-tuple-element.29.main_ref, ...), custom_call_target="tpu_custom_call" | custom-call | tf_op jit(solution)/shard_map/pallas_call | solution.py:753
  42.7 29.1 %all_to_all.15 = f32[16,16,128]{2,1,0:T(8,128)S(1)} all-to-all(f32[16,16,128]{2,1,0:T(8,128)S(1)} %get-tuple-element.32), channel_id=1, replica_groups=mesh['gx'=16,'gy'=8,'gz'=4] {'gx'}, dimensions={0} | all-to-all | bytes 262144 | tf_op jit(solution)/shard_map/all_to_all | solution.py:810
  71.9 14.2 %all_to_all.16.gathered_ref = f32[4,160,128]{2,1,0:T(8,128)S(1)} all-to-all(f32[4,160,128]{2,1,0:T(8,128)S(1)} %shard_map.32), channel_id=1, replica_groups=mesh['gx'=16,'gy'=8,'gz'=4] {'gz'}, dimensions={0} | all-to-all | bytes 655360 | tf_op jit(solution)/shard_map/all_to_all | solution.py:812
  86.1 0.3 shard_map.33.own_ref
  86.4 2.5 %collective-permute-start.7 = (f32[640,128]{1,0:T(8,128)S(1)}, f32[640,128]{1,0:T(8,128)S(1)}, u32[]{:S(2)}, u32[]{:S(2)}) collective-permute-start(f32[640,128]{1,0:T(8,128)S(1)} %shard_map.33.own_ref), channel_id=1, source_target_pairs={{0,28},{4,0},{8,4},{12,8},{16,12},{20,16},{24,20},{28,24},{1,29},{... | collective-permute-start | bytes 983048 | tf_op jit(solution)/shard_map/ppermute | solution.py:771
  88.9 0.0 collective-permute-start.6
  88.9 4.6 %collective-permute-done.7.high_ref = f32[640,128]{1,0:T(8,128)S(1)} collective-permute-done((f32[640,128]{1,0:T(8,128)S(1)}, f32[640,128]{1,0:T(8,128)S(1)}, u32[]{:S(2)}, u32[]{:S(2)}) %collective-permute-start.7) | collective-permute-done | bytes 327712 | tf_op jit(solution)/shard_map/ppermute | solution.py:771
  93.5 3.1 %collective-permute-done.6.low_ref = f32[640,128]{1,0:T(8,128)S(1)} collective-permute-done((f32[640,128]{1,0:T(8,128)S(1)}, f32[640,128]{1,0:T(8,128)S(1)}, u32[]{:S(2)}, u32[]{:S(2)}) %collective-permute-start.6) | collective-permute-done | bytes 327712 | tf_op jit(solution)/shard_map/ppermute | solution.py:771
  96.6 2.3 %shard_map.34 = (f32[4,8,128]{2,1,0:T(8,128)S(1)}, f32[8,64,128]{2,1,0:T(8,128)S(1)}) custom-call(f32[640,128]{1,0:T(8,128)S(1)} %collective-permute-done.6.low_ref, f32[640,128]{1,0:T(8,128)S(1)} %shard_map.33.own_ref, f32[640,128]{1,0:T(8,128)S(1)} %collective-permute-done.7.high_ref), custom_call_target="tpu_custom_call" | custom-call | tf_op jit(solution)/shard_map/pallas_call | solution.py:753
  98.9 9.9 %all_to_all.17.gathered_ref = f32[8,64,128]{2,1,0:T(8,128)S(1)} all-to-all(f32[8,64,128]{2,1,0:T(8,128)S(1)} %get-tuple-element.33), channel_id=1, replica_groups=mesh['gx'=16,'gy'=8,'gz'=4] {'gy'}, dimensions={0} | all-to-all | bytes 524288 | tf_op jit(solution)/shard_map/all_to_all | solution.py:823
  108.8 3.7 %shard_map.35 = f32[16,16,128]{2,1,0:T(8,128)} custom-call(f32[8,64,128]{2,1,0:T(8,128)S(1)} %all_to_all.17.gathered_ref, f32[16,16,128]{2,1,0:T(8,128)S(1)} %get-tuple-element.34.u0_ref, f32[8,8,128]{2,1,0:T(8,128)S(1)} %get-tuple-element.35.u1_ref, f32[4,8,128]{2,1,0:T(8,128)S(1)} %get-tuple-element.36.u2_ref), custom_call_target="tpu_custom_call" | custom-call | tf_op jit(solution)/shard_map/pallas_call | solution.py:753
  (3 shorter events, 0.1 us)
Async XLA Ops:
  0.0 0.9 copy-start
  0.9 0.9 copy-start.2
  1.8 12.6 %copy-start.1 = (f32[16,16,128]{2,1,0:T(8,128)S(1)}, f32[16,16,128]{2,1,0:T(8,128)}, u32[]{:S(2)}) copy-start(f32[16,16,128]{2,1,0:T(8,128)} %f_ref.3) | copy-start | bytes 393220
  1.8 12.6 %copy-start.3 = (f32[16,16,128]{2,1,0:T(8,128)S(1)}, f32[16,16,128]{2,1,0:T(8,128)}, u32[]{:S(2)}) copy-start(f32[16,16,128]{2,1,0:T(8,128)} %b_ref.3) | copy-start | bytes 393220
  1.8 10.6 %collective-permute-start = (f32[25,16,128]{2,1,0:T(8,128)S(1)}, f32[25,16,128]{2,1,0:T(8,128)S(1)}, u32[]{:S(2)}, u32[]{:S(2)}) collective-permute-start(f32[25,16,128]{2,1,0:T(8,128)S(1)} %get-tuple-element.21), channel_id=1, source_target_pairs={{0,32},{32,64},{64,96},{96,128},{128,160},{160,192},{192,224},{224... | collective-permute-start | bytes 614408 | tf_op jit(solution)/shard_map/ppermute | solution.py:766
  5.8 8.6 %collective-permute-start.1 = (f32[25,16,128]{2,1,0:T(8,128)S(1)}, f32[25,16,128]{2,1,0:T(8,128)S(1)}, u32[]{:S(2)}, u32[]{:S(2)}) collective-permute-start(f32[25,16,128]{2,1,0:T(8,128)S(1)} %get-tuple-element.22), channel_id=1, source_target_pairs={{32,0},{64,32},{96,64},{128,96},{160,128},{192,160},{224,192},{256... | collective-permute-start | bytes 614408 | tf_op jit(solution)/shard_map/ppermute | solution.py:766
  14.7 6.4 %collective-permute-start.2 = (f32[11,16,128]{2,1,0:T(8,128)S(1)}, f32[11,16,128]{2,1,0:T(8,128)S(1)}, u32[]{:S(2)}, u32[]{:S(2)}) collective-permute-start(f32[11,16,128]{2,1,0:T(8,128)S(1)} %get-tuple-element.25), channel_id=1, source_target_pairs={{0,1},{2,3},{1,0},{3,2},{4,5},{6,7},{5,4},{7,6},{8,9},{10,11},{9,8... | collective-permute-start | bytes 270344 | tf_op jit(solution)/shard_map/ppermute | solution.py:778
  18.1 3.0 %collective-permute-start.3 = (f32[11,16,128]{2,1,0:T(8,128)S(1)}, f32[11,16,128]{2,1,0:T(8,128)S(1)}, u32[]{:S(2)}, u32[]{:S(2)}) collective-permute-start(f32[11,16,128]{2,1,0:T(8,128)S(1)} %get-tuple-element.26), channel_id=1, source_target_pairs={{1,2},{2,1},{5,6},{6,5},{9,10},{10,9},{13,14},{14,13},{17,18},{18,... | collective-permute-start | bytes 270344 | tf_op jit(solution)/shard_map/ppermute | solution.py:778
  21.2 9.4 %collective-permute-start.4 = (f32[944,128]{1,0:T(8,128)S(1)}, f32[944,128]{1,0:T(8,128)S(1)}, u32[]{:S(2)}, u32[]{:S(2)}) collective-permute-start(f32[944,128]{1,0:T(8,128)S(1)} %get-tuple-element.27), channel_id=1, source_target_pairs={{0,4},{4,8},{8,12},{12,16},{16,20},{20,24},{24,28},{28,0},{1,5},{5... | collective-permute-start | bytes 1449992 | tf_op jit(solution)/shard_map/ppermute | solution.py:771
  21.2 9.4 %collective-permute-start.5 = (f32[944,128]{1,0:T(8,128)S(1)}, f32[944,128]{1,0:T(8,128)S(1)}, u32[]{:S(2)}, u32[]{:S(2)}) collective-permute-start(f32[944,128]{1,0:T(8,128)S(1)} %get-tuple-element.28), channel_id=1, source_target_pairs={{0,28},{4,0},{8,4},{12,8},{16,12},{20,16},{24,20},{28,24},{1,29},{... | collective-permute-start | bytes 1449992 | tf_op jit(solution)/shard_map/ppermute | solution.py:771
  86.4 7.1 %collective-permute-start.7 = (f32[640,128]{1,0:T(8,128)S(1)}, f32[640,128]{1,0:T(8,128)S(1)}, u32[]{:S(2)}, u32[]{:S(2)}) collective-permute-start(f32[640,128]{1,0:T(8,128)S(1)} %shard_map.33.own_ref), channel_id=1, source_target_pairs={{0,28},{4,0},{8,4},{12,8},{16,12},{20,16},{24,20},{28,24},{1,29},{... | collective-permute-start | bytes 983048 | tf_op jit(solution)/shard_map/ppermute | solution.py:771
  88.9 7.7 %collective-permute-start.6 = (f32[640,128]{1,0:T(8,128)S(1)}, f32[640,128]{1,0:T(8,128)S(1)}, u32[]{:S(2)}, u32[]{:S(2)}) collective-permute-start(f32[640,128]{1,0:T(8,128)S(1)} %shard_map.33.own_ref), channel_id=1, source_target_pairs={{0,4},{4,8},{8,12},{12,16},{16,20},{20,24},{24,28},{28,0},{1,5},{5... | collective-permute-start | bytes 983048 | tf_op jit(solution)/shard_map/ppermute | solution.py:771

commit v5 on v4

--- a/solution.py
+++ b/solution.py
@@ -27,7 +27,7 @@
 OFFSETS = [sum(COUNTS[:index]) for index in range(PLANES)]
 PACKED = sum(COUNTS)
 STRIP_ROWS = [
-    8 * -(-max(0, max(COUNTS[8 * group : 8 * group + 8]) - 1) // 8) for group in range(GROUPS)
+    max(0, max(COUNTS[8 * group : 8 * group + 8]) - 1) for group in range(GROUPS)
 ]
 STRIP_OFFSETS = [PACKED + sum(STRIP_ROWS[:group]) for group in range(GROUPS)]
 SIDE = sum(STRIP_ROWS)
@@ -235,13 +235,6 @@
     return ref[pl.ds(0, rows, stride=2), :] + ref[pl.ds(1, rows, stride=2), :]
 
 
-def edge_kernel(f_ref, b_ref, upper_ref, lower_ref):
-    upper_ref[0:F_HALO] = f_ref[BLOCK - F_HALO : BLOCK]
-    upper_ref[F_HALO:] = b_ref[BLOCK - B_HALO : BLOCK]
-    lower_ref[0:F_HALO] = f_ref[0:F_HALO]
-    lower_ref[F_HALO:] = b_ref[0:B_HALO]
-
-
 def pack_kernel(
     f_ref, b_ref, low_ref, high_ref, main_ref, left_ref, right_ref, down_ref, up_ref
 ):
@@ -460,7 +453,7 @@
             out_ref[index, 16 * row : 16 * row + 16] = value
 
 
-def line_kernel(gathered_ref, out_ref):
+def line_kernel(gathered_ref, out_ref, up_ref, down_ref):
     group = iota((16, 128), 1) >> 5
     for row in range(10):
         here = slice(16 * row, 16 * row + 16)
@@ -473,6 +466,11 @@
                     value = jnp.where(group == position, moved, value)
             start = 64 * row + 16 * part
             out_ref[start : start + 16] = value
+            if row < 9:
+                up_ref[start : start + 16] = value
+            if row != 4:
+                start -= 64 * (row > 4)
+                down_ref[start : start + 16] = value
 
 
 class Blocks(Level):
@@ -511,7 +509,7 @@
         put(b, 5 + index, own_ref, 5 + index)
     for index in range(5):
         put(b, index, low_ref, 4 + index, low_there)
-        put(b, 9 + index, high_ref, 5 + index, high_there)
+        put(b, 9 + index, high_ref, 4 + index, high_there)
 
     zero = jnp.zeros((8, 128), F32)
     for refs in (column.b, column.fy, column.r, column.k):
@@ -780,8 +778,8 @@
 
 def on_device(right_side, conductivity):
     f, b = right_side, conductivity
-    edge = (F_HALO + B_HALO, BLOCK, 128)
-    upper, lower = call(edge_kernel, 2, [edge, edge], [], f, b)
+    upper = jnp.concatenate([f[BLOCK - F_HALO :], b[BLOCK - B_HALO :]], axis=0)
+    lower = jnp.concatenate([f[:F_HALO], b[:B_HALO]], axis=0)
     low, high = shift(upper, "gx", 1), shift(lower, "gx", -1)
 
     strip = (GROUPS, BLOCK, 128)
@@ -810,8 +808,8 @@
     column = lax.all_to_all(coarse, "gx", 0, 0, tiled=True)
     (column,) = call(squeeze_kernel, 2, [(4, 160, 128)], [], column.reshape(256, 128))
     column = lax.all_to_all(column, "gz", 0, 0, tiled=True)
-    (column,) = call(line_kernel, 2, [(640, 128)], [], column)
-    low, high = around(column, "gy", 1), around(column, "gy", -1)
+    column, up, down = call(line_kernel, 4, [(640, 128), (576, 128), (576, 128)], [], column)
+    low, high = around(up, "gy", 1), around(down, "gy", -1)
     u2, coarse = call(
         column_kernel,
         13,

time: 113 us -> 111 us (0.982)
  the two profiles are of different devices: /device:TPU:32 before, /device:TPU:1 now
where the time goes in v5:
time: 111 us
  blocking collectives  50.5 us (45%)
  waiting for transfers between devices  20.5 us (18%)
  starting transfers between devices  19.6 us (18%)
  Pallas kernels  18.8 us (17%)
    all_to_all x1, blocking collectives, on_device(): column = lax.all_to_all(coarse, 'gx', 0, 0, tiled=True)  26.5 us
    pallas_call x7, Pallas kernels, call(): pl.pallas_call(kernel, out_shape=[jax.ShapeDtypeStruct(shape, F32) for sh...  18.8 us
    ppermute x4, waiting for transfers between devices, around(): lax.ppermute(value, axis, [(i, (i + step) % count) for i in range(count)])  13.8 us
    all_to_all x1, blocking collectives, on_device(): column = lax.all_to_all(column, 'gz', 0, 0, tiled=True)  12.8 us
    all_to_all x1, blocking collectives, on_device(): whole = lax.all_to_all(coarse, 'gy', 0, 0, tiled=True)  11.2 us
    ppermute x4, starting transfers between devices, around(): lax.ppermute(value, axis, [(i, (i + step) % count) for i in range(count)])  8.8 us
    ppermute x2, starting transfers between devices, shift(): return lax.ppermute(value, axis, pairs)  5.8 us
    ppermute x2, waiting for transfers between devices, shift(): return lax.ppermute(value, axis, pairs)  5.38 us
  transfers between devices with their start and end apart: 8, of which 7 were waited for; matrix products, arithmetic and copies ran while one was open for 0% of the time, Pallas kernels for 0%

profile of v5, /device:TPU:1, one launch (start us, length us, event | category | flops | bytes accessed | tf_op | source)
XLA Modules:
  0.0 110.6 jit_solution(4233399936190859558)
XLA Ops:
  0.0 0.0 copy-start
  0.0 1.0 fusion
  1.0 0.0 copy-done
  1.1 4.4 %collective-permute-start = (f32[25,16,128]{2,1,0:T(8,128)S(1)}, f32[25,16,128]{2,1,0:T(8,128)S(1)}, u32[]{:S(2)}, u32[]{:S(2)}) collective-permute-start(f32[25,16,128]{2,1,0:T(8,128)S(1)} %pad_maximum_fusion), channel_id=1, source_target_pairs={{0,32},{32,64},{64,96},{96,128},{128,160},{160,192},{192,224},{224... | collective-permute-start | bytes 614408 | tf_op jit(solution)/shard_map/ppermute | solution.py:764
  5.4 0.0 copy-start.1
  5.5 1.4 %collective-permute-start.1 = (f32[25,16,128]{2,1,0:T(8,128)S(1)}, f32[25,16,128]{2,1,0:T(8,128)S(1)}, u32[]{:S(2)}, u32[]{:S(2)}) collective-permute-start(f32[25,16,128]{2,1,0:T(8,128)S(1)} %pad_maximum_fusion.1), channel_id=1, source_target_pairs={{32,0},{64,32},{96,64},{128,96},{160,128},{192,160},{224,192},{256... | collective-permute-start | bytes 614408 | tf_op jit(solution)/shard_map/ppermute | solution.py:764
  6.9 1.2 %collective-permute-done.low_ref = f32[25,16,128]{2,1,0:T(8,128)S(1)} collective-permute-done((f32[25,16,128]{2,1,0:T(8,128)S(1)}, f32[25,16,128]{2,1,0:T(8,128)S(1)}, u32[]{:S(2)}, u32[]{:S(2)}) %collective-permute-start) | collective-permute-done | bytes 204832 | tf_op jit(solution)/shard_map/ppermute | solution.py:764
  8.1 4.2 %collective-permute-done.1.high_ref = f32[25,16,128]{2,1,0:T(8,128)S(1)} collective-permute-done((f32[25,16,128]{2,1,0:T(8,128)S(1)}, f32[25,16,128]{2,1,0:T(8,128)S(1)}, u32[]{:S(2)}, u32[]{:S(2)}) %collective-permute-start.1) | collective-permute-done | bytes 204832 | tf_op jit(solution)/shard_map/ppermute | solution.py:764
  12.3 0.0 copy-done.1
  12.3 0.2 shard_map.28
  12.5 4.4 %collective-permute-start.2 = (f32[11,16,128]{2,1,0:T(8,128)S(1)}, f32[11,16,128]{2,1,0:T(8,128)S(1)}, u32[]{:S(2)}, u32[]{:S(2)}) collective-permute-start(f32[11,16,128]{2,1,0:T(8,128)S(1)} %get-tuple-element.24), channel_id=1, source_target_pairs={{0,1},{2,3},{1,0},{3,2},{4,5},{6,7},{5,4},{7,6},{8,9},{10,11},{9,8... | collective-permute-start | bytes 270344 | tf_op jit(solution)/shard_map/ppermute | solution.py:776
  16.9 0.7 collective-permute-start.3
  17.6 1.2 %collective-permute-done.2.first_ref = f32[11,16,128]{2,1,0:T(8,128)S(1)} collective-permute-done((f32[11,16,128]{2,1,0:T(8,128)S(1)}, f32[11,16,128]{2,1,0:T(8,128)S(1)}, u32[]{:S(2)}, u32[]{:S(2)}) %collective-permute-start.2) | collective-permute-done | bytes 90144 | tf_op jit(solution)/shard_map/ppermute | solution.py:776
  18.8 0.0 collective-permute-done.3.second_ref
  18.8 0.1 shard_map.29
  18.9 4.2 %collective-permute-start.4 = (f32[878,128]{1,0:T(8,128)S(1)}, f32[878,128]{1,0:T(8,128)S(1)}, u32[]{:S(2)}, u32[]{:S(2)}) collective-permute-start(f32[878,128]{1,0:T(8,128)S(1)} %get-tuple-element.26), channel_id=1, source_target_pairs={{0,4},{4,8},{8,12},{12,16},{16,20},{20,24},{24,28},{28,0},{1,5},{5... | collective-permute-start | bytes 1348616 | tf_op jit(solution)/shard_map/ppermute | solution.py:769
  23.1 0.7 collective-permute-start.5
  23.8 4.6 %collective-permute-done.4.low_ref = f32[878,128]{1,0:T(8,128)S(1)} collective-permute-done((f32[878,128]{1,0:T(8,128)S(1)}, f32[878,128]{1,0:T(8,128)S(1)}, u32[]{:S(2)}, u32[]{:S(2)}) %collective-permute-start.4) | collective-permute-done | bytes 449568 | tf_op jit(solution)/shard_map/ppermute | solution.py:769
  28.5 2.8 %collective-permute-done.5.high_ref = f32[878,128]{1,0:T(8,128)S(1)} collective-permute-done((f32[878,128]{1,0:T(8,128)S(1)}, f32[878,128]{1,0:T(8,128)S(1)}, u32[]{:S(2)}, u32[]{:S(2)}) %collective-permute-start.5) | collective-permute-done | bytes 449568 | tf_op jit(solution)/shard_map/ppermute | solution.py:769
  31.2 12.2 %shard_map.30 = (f32[16,16,128]{2,1,0:T(8,128)S(1)}, f32[8,8,128]{2,1,0:T(8,128)S(1)}, f32[16,16,128]{2,1,0:T(8,128)S(1)}) custom-call(f32[878,128]{1,0:T(8,128)S(1)} %collective-permute-done.4.low_ref, f32[878,128]{1,0:T(8,128)S(1)} %collective-permute-done.5.high_ref, f32[82,16,128]{2,1,0:T(8,128)S(1)} %get-tuple-element.28.main_ref, ...), custom_call_target="tpu_custom_call" | custom-call | tf_op jit(solution)/shard_map/pallas_call | solution.py:751
  43.4 26.5 %all_to_all.15 = f32[16,16,128]{2,1,0:T(8,128)S(1)} all-to-all(f32[16,16,128]{2,1,0:T(8,128)S(1)} %get-tuple-element.31), channel_id=1, replica_groups=mesh['gx'=16,'gy'=8,'gz'=4] {'gx'}, dimensions={0} | all-to-all | bytes 262144 | tf_op jit(solution)/shard_map/all_to_all | solution.py:808
  69.9 12.8 %all_to_all.16.gathered_ref = f32[4,160,128]{2,1,0:T(8,128)S(1)} all-to-all(f32[4,160,128]{2,1,0:T(8,128)S(1)} %shard_map.31), channel_id=1, replica_groups=mesh['gx'=16,'gy'=8,'gz'=4] {'gz'}, dimensions={0} | all-to-all | bytes 655360 | tf_op jit(solution)/shard_map/all_to_all | solution.py:810
  82.7 0.3 shard_map.32
  83.0 3.9 %collective-permute-start.6 = (f32[576,128]{1,0:T(8,128)S(1)}, f32[576,128]{1,0:T(8,128)S(1)}, u32[]{:S(2)}, u32[]{:S(2)}) collective-permute-start(f32[576,128]{1,0:T(8,128)S(1)} %get-tuple-element.32), channel_id=1, source_target_pairs={{0,4},{4,8},{8,12},{12,16},{16,20},{20,24},{24,28},{28,0},{1,5},{5... | collective-permute-start | bytes 884744 | tf_op jit(solution)/shard_map/ppermute | solution.py:769
  86.9 0.0 collective-permute-start.7
  86.9 3.7 %collective-permute-done.6.low_ref = f32[576,128]{1,0:T(8,128)S(1)} collective-permute-done((f32[576,128]{1,0:T(8,128)S(1)}, f32[576,128]{1,0:T(8,128)S(1)}, u32[]{:S(2)}, u32[]{:S(2)}) %collective-permute-start.6) | collective-permute-done | bytes 294944 | tf_op jit(solution)/shard_map/ppermute | solution.py:769
  90.6 2.8 %collective-permute-done.7.high_ref = f32[576,128]{1,0:T(8,128)S(1)} collective-permute-done((f32[576,128]{1,0:T(8,128)S(1)}, f32[576,128]{1,0:T(8,128)S(1)}, u32[]{:S(2)}, u32[]{:S(2)}) %collective-permute-start.7) | collective-permute-done | bytes 294944 | tf_op jit(solution)/shard_map/ppermute | solution.py:769
  93.3 2.3 %shard_map.33 = (f32[4,8,128]{2,1,0:T(8,128)S(1)}, f32[8,64,128]{2,1,0:T(8,128)S(1)}) custom-call(f32[576,128]{1,0:T(8,128)S(1)} %collective-permute-done.6.low_ref, f32[640,128]{1,0:T(8,128)S(1)} %get-tuple-element.33.own_ref, f32[576,128]{1,0:T(8,128)S(1)} %collective-permute-done.7.high_ref), custom_call_target="tpu_custom_call" | custom-call | tf_op jit(solution)/shard_map/pallas_call | solution.py:751
  95.6 11.2 %all_to_all.17.gathered_ref = f32[8,64,128]{2,1,0:T(8,128)S(1)} all-to-all(f32[8,64,128]{2,1,0:T(8,128)S(1)} %get-tuple-element.35), channel_id=1, replica_groups=mesh['gx'=16,'gy'=8,'gz'=4] {'gy'}, dimensions={0} | all-to-all | bytes 524288 | tf_op jit(solution)/shard_map/all_to_all | solution.py:821
  106.8 3.7 %shard_map.34 = f32[16,16,128]{2,1,0:T(8,128)} custom-call(f32[8,64,128]{2,1,0:T(8,128)S(1)} %all_to_all.17.gathered_ref, f32[16,16,128]{2,1,0:T(8,128)S(1)} %get-tuple-element.36.u0_ref, f32[8,8,128]{2,1,0:T(8,128)S(1)} %get-tuple-element.37.u1_ref, f32[4,8,128]{2,1,0:T(8,128)S(1)} %get-tuple-element.38.u2_ref), custom_call_target="tpu_custom_call" | custom-call | tf_op jit(solution)/shard_map/pallas_call | solution.py:751
  (4 shorter events, 0.1 us)
Async XLA Ops:
  0.0 1.0 copy-start
  1.1 7.1 %collective-permute-start = (f32[25,16,128]{2,1,0:T(8,128)S(1)}, f32[25,16,128]{2,1,0:T(8,128)S(1)}, u32[]{:S(2)}, u32[]{:S(2)}) collective-permute-start(f32[25,16,128]{2,1,0:T(8,128)S(1)} %pad_maximum_fusion), channel_id=1, source_target_pairs={{0,32},{32,64},{64,96},{96,128},{128,160},{160,192},{192,224},{224... | collective-permute-start | bytes 614408 | tf_op jit(solution)/shard_map/ppermute | solution.py:764
  5.4 6.8 %copy-start.1 = (f32[16,16,128]{2,1,0:T(8,128)S(1)}, f32[16,16,128]{2,1,0:T(8,128)}, u32[]{:S(2)}) copy-start(f32[16,16,128]{2,1,0:T(8,128)} %f_ref.1) | copy-start | bytes 393220
  5.5 6.8 %collective-permute-start.1 = (f32[25,16,128]{2,1,0:T(8,128)S(1)}, f32[25,16,128]{2,1,0:T(8,128)S(1)}, u32[]{:S(2)}, u32[]{:S(2)}) collective-permute-start(f32[25,16,128]{2,1,0:T(8,128)S(1)} %pad_maximum_fusion.1), channel_id=1, source_target_pairs={{32,0},{64,32},{96,64},{128,96},{160,128},{192,160},{224,192},{256... | collective-permute-start | bytes 614408 | tf_op jit(solution)/shard_map/ppermute | solution.py:764
  12.5 6.3 %collective-permute-start.2 = (f32[11,16,128]{2,1,0:T(8,128)S(1)}, f32[11,16,128]{2,1,0:T(8,128)S(1)}, u32[]{:S(2)}, u32[]{:S(2)}) collective-permute-start(f32[11,16,128]{2,1,0:T(8,128)S(1)} %get-tuple-element.24), channel_id=1, source_target_pairs={{0,1},{2,3},{1,0},{3,2},{4,5},{6,7},{5,4},{7,6},{8,9},{10,11},{9,8... | collective-permute-start | bytes 270344 | tf_op jit(solution)/shard_map/ppermute | solution.py:776
  16.9 1.9 %collective-permute-start.3 = (f32[11,16,128]{2,1,0:T(8,128)S(1)}, f32[11,16,128]{2,1,0:T(8,128)S(1)}, u32[]{:S(2)}, u32[]{:S(2)}) collective-permute-start(f32[11,16,128]{2,1,0:T(8,128)S(1)} %get-tuple-element.25), channel_id=1, source_target_pairs={{1,2},{2,1},{5,6},{6,5},{9,10},{10,9},{13,14},{14,13},{17,18},{18,... | collective-permute-start | bytes 270344 | tf_op jit(solution)/shard_map/ppermute | solution.py:776
  18.9 9.6 %collective-permute-start.4 = (f32[878,128]{1,0:T(8,128)S(1)}, f32[878,128]{1,0:T(8,128)S(1)}, u32[]{:S(2)}, u32[]{:S(2)}) collective-permute-start(f32[878,128]{1,0:T(8,128)S(1)} %get-tuple-element.26), channel_id=1, source_target_pairs={{0,4},{4,8},{8,12},{12,16},{16,20},{20,24},{24,28},{28,0},{1,5},{5... | collective-permute-start | bytes 1348616 | tf_op jit(solution)/shard_map/ppermute | solution.py:769
  23.1 8.1 %collective-permute-start.5 = (f32[878,128]{1,0:T(8,128)S(1)}, f32[878,128]{1,0:T(8,128)S(1)}, u32[]{:S(2)}, u32[]{:S(2)}) collective-permute-start(f32[878,128]{1,0:T(8,128)S(1)} %get-tuple-element.27), channel_id=1, source_target_pairs={{0,28},{4,0},{8,4},{12,8},{16,12},{20,16},{24,20},{28,24},{1,29},{... | collective-permute-start | bytes 1348616 | tf_op jit(solution)/shard_map/ppermute | solution.py:769
  83.0 7.5 %collective-permute-start.6 = (f32[576,128]{1,0:T(8,128)S(1)}, f32[576,128]{1,0:T(8,128)S(1)}, u32[]{:S(2)}, u32[]{:S(2)}) collective-permute-start(f32[576,128]{1,0:T(8,128)S(1)} %get-tuple-element.32), channel_id=1, source_target_pairs={{0,4},{4,8},{8,12},{12,16},{16,20},{20,24},{24,28},{28,0},{1,5},{5... | collective-permute-start | bytes 884744 | tf_op jit(solution)/shard_map/ppermute | solution.py:769
  86.9 6.4 %collective-permute-start.7 = (f32[576,128]{1,0:T(8,128)S(1)}, f32[576,128]{1,0:T(8,128)S(1)}, u32[]{:S(2)}, u32[]{:S(2)}) collective-permute-start(f32[576,128]{1,0:T(8,128)S(1)} %get-tuple-element.34), channel_id=1, source_target_pairs={{0,28},{4,0},{8,4},{12,8},{16,12},{20,16},{24,20},{28,24},{1,29},{... | collective-permute-start | bytes 884744 | tf_op jit(solution)/shard_map/ppermute | solution.py:769
